TPU v7x, 256 devices: a whole 4x4x8 slice. The times are simulated.
256 devices in a mesh: tiles: 64 (over y, x_lo, z), probes: 4 (over x_hi, core).
Axes of the slice: x: 4 (x_hi: 2, x_lo: 2; x = x_hi * 2 + x_lo), y: 4, z: 8, core: 2. Of those that a mesh axis runs over, the one named last changes fastest.
Arguments:
- blocks: bfloat16 [4096, 192, 192], P('tiles'), may hold values from -0.21875 to 0.21875
- connectivity: int32 [4096, 64], P('tiles'), may hold values from 0 to 4607, as said below
- basal_map: int32 [4096, 64], P('tiles'), may hold values from 0 to 383
- friction: float32 [4096, 64, 3], P('tiles'), may hold values from 0.2 to 2
- elem_counts: int32 [64], P('tiles'), may hold values from 1 to 64, 3072 in all
- obs_weight: float32 [262144, 3], P('tiles'), may hold values from 0.2 to 2
- sign_bits: int32 [16384, 32], P('tiles', 'probes'), may hold values from 0 to 1
- cluster_ids: int32 [16384], P('tiles'), may hold values from 0 to 63, never falling along the last dimension, each value on 1 to 512 neighbouring positions
Outputs:
- samples: float32 [16384, 32], P('tiles', 'probes')
- refined: float32 [16384, 32], P('tiles', 'probes')
- gram: float32 [64, 32, 32], P(None, 'probes')
Inputs may be any that keep to these rules, and one draw needn't show every extreme that they name: `connectivity`: about one reference in eight names a node of the next tile. `elem_counts`: some tile has all 64 slots live. `cluster_ids`: never falling along the cells; each cluster holds 1 to 512 cells.
All inputs are finite; a program needn't handle non-finite values. No bound on the sum of `elem_counts` on one device may be relied on, other than what follows from the above.
Results may differ from a plain program's by a relative error of at most 0.004.
Values may be sent and summed in bfloat16 or wider, within the bound.
A program may use at most 64 MiB of HBM per device.

v0:
```python
import jax
import jax.numpy as jnp
from jax import lax
from jax.sharding import PartitionSpec as P

HALO = 512
POWER = 2
RIM = 64


def padded(x, sides, width):
    for axis, dim in sides:
        size, length = (lax.axis_size(axis), x.shape[dim])
        up = [(i, (i + 1) % size) for i in range(size - 1)]
        down = [(j, i) for i, j in up]
        last = lax.slice_in_dim(x, length - width, length, axis=dim)
        leading = lax.slice_in_dim(x, 0, width, axis=dim)
        before = lax.ppermute(last, axis, up)
        after = lax.ppermute(leading, axis, down)
        x = jnp.concatenate([before, x, after], axis=dim)
    return x


def from_behind(block, axis, distance):
    devices = range(lax.axis_size(axis))
    route = [(i - distance, i) for i in devices if i - distance in devices]
    return lax.ppermute(block, axis, route)


def shards(
    blocks, connectivity, basal_map, friction, elem_counts, obs_weight, sign_bits, cluster_ids
):
    elem_slots = blocks.shape[0]
    block_order = blocks.shape[1]
    node_slots = connectivity.shape[1]
    node_count = obs_weight.shape[0]
    halo_nodes = HALO
    rim_cells = RIM
    cell_count = sign_bits.shape[0]
    group_size = sign_bits.shape[1]
    tile_count = lax.axis_size("tiles")
    alive_slots = jnp.arange(elem_slots, dtype=jnp.int32) < elem_counts[0]
    flat_nodes = connectivity.reshape(-1)
    flat_cells = basal_map.reshape(-1)

    def hessian(probe_field):
        window = padded(probe_field, (("tiles", 0),), rim_cells)
        picked = window[basal_map]
        inputs = (friction[:, :, :, None] * picked[:, :, None, :]).astype(jnp.bfloat16)
        inputs = inputs.reshape(elem_slots, block_order, group_size)
        forward = jnp.einsum("eij,ejp->eip", blocks, inputs, preferred_element_type=jnp.float32)
        forward = jnp.where(alive_slots[:, None, None], forward, jnp.float32(0.0))
        summed = jax.ops.segment_sum(
            forward.reshape(elem_slots * node_slots, 3 * group_size),
            flat_nodes,
            num_segments=node_count + halo_nodes,
        )
        owned_sum = summed[:node_count]
        spilled = summed[node_count:]
        returned = from_behind(spilled, "tiles", 1)
        owned_sum = jnp.concatenate([owned_sum[:halo_nodes] + returned, owned_sum[halo_nodes:]], 0)
        weighted = (obs_weight[:, :, None] * owned_sum.reshape(node_count, 3, group_size)).astype(
            jnp.bfloat16
        )
        weighted = weighted.reshape(node_count, 3 * group_size)
        weighted_rim = from_behind(weighted[:halo_nodes], "tiles", -1)
        node_window = jnp.concatenate([weighted, weighted_rim], 0)
        adjoint_in = node_window[connectivity].reshape(elem_slots, block_order, group_size)
        adjoint_out = jnp.einsum(
            "eji,ejp->eip", blocks, adjoint_in, preferred_element_type=jnp.float32
        )
        partials = jnp.sum(
            friction[:, :, :, None] * adjoint_out.reshape(elem_slots, node_slots, 3, group_size),
            axis=2,
        )
        partials = jnp.where(alive_slots[:, None, None], partials, jnp.float32(0.0))
        basal = jax.ops.segment_sum(
            partials.reshape(elem_slots * node_slots, group_size),
            flat_cells,
            num_segments=cell_count + 2 * rim_cells,
        )
        from_next = from_behind(basal[:rim_cells], "tiles", -1)
        from_prev = from_behind(basal[cell_count + rim_cells :], "tiles", 1)
        middle = basal[rim_cells : cell_count + rim_cells]
        middle = middle + jnp.pad(from_prev, ((0, cell_count - rim_cells), (0, 0)))
        middle = middle + jnp.pad(from_next, ((cell_count - rim_cells, 0), (0, 0)))
        return middle

    parity = jnp.arange(group_size, dtype=jnp.int32) % 2
    same_colour = (cluster_ids % 2)[:, None] == parity[None, :]
    probe_start = jnp.where(same_colour, (2 * sign_bits - 1).astype(jnp.float32), jnp.float32(0.0))
    samples = jnp.where(same_colour, jnp.float32(0.0), hessian(probe_start))
    current = samples
    for power_step in range(POWER):
        squares = lax.psum(jnp.sum(current * current, axis=0), "tiles")
        rms_scale = jnp.sqrt(squares / (cell_count * tile_count) + 1e-06)
        applied = hessian(current / rms_scale)
        if power_step % 2 == 0:
            current = jnp.where(same_colour, applied, jnp.float32(0.0))
        else:
            current = jnp.where(same_colour, jnp.float32(0.0), applied)
    onehot = (cluster_ids[:, None] == jnp.arange(tile_count, dtype=jnp.int32)[None, :]).astype(
        jnp.float32
    )
    column_block = lax.all_gather(current, "probes", axis=1, tiled=True)
    outer = current[:, :, None] * column_block[:, None, :]
    width = column_block.shape[1]
    result = jnp.dot(
        onehot.T, outer.reshape(cell_count, group_size * width), precision=lax.Precision.HIGHEST
    )
    partial_gram = result.reshape(tile_count, group_size, width)
    gram = lax.psum(partial_gram, "tiles")
    return (samples, current, gram)


def solution(mesh):
    in_specs = (
        P("tiles", None, None),
        P("tiles", None),
        P("tiles", None),
        P("tiles", None, None),
        P("tiles"),
        P("tiles", None),
        P("tiles", "probes"),
        P("tiles"),
    )
    out_specs = (P("tiles", "probes"), P("tiles", "probes"), P(None, "probes", None))
    return jax.shard_map(shards, mesh=mesh, in_specs=in_specs, out_specs=out_specs, check_vma=False)
```

profile of v0, /device:TPU:2, one launch (start us, length us, event | category | flops | bytes accessed | tf_op | source)
XLA Modules:
  0.0 1260.6 jit_solution(13736577192659652602)
XLA Ops:
  8.8 3.8 collective-permute-start
  12.6 5.8 collective-permute-start.1
  22.0 10.8 gather_fusion
  34.3 4.5 fusion.2
  38.8 4.1 copy.177
  42.9 5.3 reshape.163
  48.1 23.2 %scatter_custom_fusion = f32[4608,24]{1,0:T(8,128)S(1)} fusion(s32[4096]{0:T(1024)S(1)} %reshape.161, f32[4096,24]{1,0:T(8,128)} %reshape.163, f32[]{:T(128)} %constant.39.clone.1), kind=kCustom, calls=%fused_computation.25 | custom fusion | flops 98304 | bytes 442880 | tf_op jit(solution)/shard_map/scatter-add | solution.py:53
  74.8 2.0 copy.179
  76.8 6.4 collective-permute-done.2
  86.6 3.5 collective-permute-done.3
  90.7 14.9 %gather_fusion.1 = bf16[4096,24]{1,0:T(8,128)(2,1)} fusion(bf16[4608,24]{1,0:T(8,128)(2,1)S(1)} %copy.180, s32[4096]{0:T(1024)S(1)} %broadcast_clamp_fusion), kind=kCustom, calls=%fused_computation.1 | custom fusion | bytes 409600 | tf_op jit(solution)/shard_map/gather | solution.py:68
  105.6 3.7 reshape.101
  109.3 4.6 convolution_bitcast_fusion.2
  116.3 22.4 %scatter_custom_fusion.1 = f32[384,8]{1,0:T(8,128)S(1)} fusion(s32[4096]{0:T(1024)S(1)} %reshape.169, f32[4096,8]{1,0:T(8,128)S(1)} %copy.184, f32[]{:T(128)} %constant.39.clone.1), kind=kCustom, calls=%fused_computation.63 | custom fusion | flops 32768 | bytes 12292 | tf_op jit(solution)/shard_map/scatter-add | solution.py:77
  138.8 4.0 collective-permute-start.5
  144.9 5.6 collective-permute-done.4
  150.7 136.6 %psum.21 = f32[8]{0:T(128)S(1)} all-reduce(f32[8]{0:T(128)S(1)} %get-tuple-element.15), channel_id=1, replica_groups=mesh['tiles'=64,'probes'=4] {'tiles'}, use_global_device_ids=true, to_apply=%region_4.5 | all-reduce | flops 8 | bytes 64 | tf_op jit(solution)/shard_map/psum | solution.py:95
  289.3 6.2 collective-permute-start.7
  296.9 10.8 gather_fusion.2
  309.2 4.5 fusion.1
  313.7 4.1 copy.191
  317.7 5.3 reshape.179
  323.0 23.2 %scatter_custom_fusion.2 = f32[4608,24]{1,0:T(8,128)S(1)} fusion(s32[4096]{0:T(1024)S(1)} %reshape.161, f32[4096,24]{1,0:T(8,128)} %reshape.179, f32[]{:T(128)} %constant.39.clone.1), kind=kCustom, calls=%fused_computation.23 | custom fusion | flops 98304 | bytes 442880 | tf_op jit(solution)/shard_map/scatter-add | solution.py:53
  351.6 5.4 collective-permute-done.8
  358.2 3.9 collective-permute-start.9
  364.4 14.9 %gather_fusion.3 = bf16[4096,24]{1,0:T(8,128)(2,1)} fusion(bf16[4608,24]{1,0:T(8,128)(2,1)S(1)} %copy.194, s32[4096]{0:T(1024)S(1)} %broadcast_clamp_fusion), kind=kCustom, calls=%fused_computation.3 | custom fusion | bytes 409600 | tf_op jit(solution)/shard_map/gather | solution.py:68
  379.3 3.7 reshape.105
  383.1 4.6 convolution_bitcast_fusion.1
  390.0 22.4 %scatter_custom_fusion.3 = f32[384,8]{1,0:T(8,128)S(1)} fusion(s32[4096]{0:T(1024)S(1)} %reshape.169, f32[4096,8]{1,0:T(8,128)S(1)} %copy.198, f32[]{:T(128)} %constant.39.clone.1), kind=kCustom, calls=%fused_computation.61 | custom fusion | flops 32768 | bytes 12292 | tf_op jit(solution)/shard_map/scatter-add | solution.py:77
  412.6 6.0 collective-permute-start.11
  420.6 5.6 collective-permute-done.10
  426.4 143.6 %psum.22 = f32[8]{0:T(128)S(1)} all-reduce(f32[8]{0:T(128)S(1)} %multiply_reduce_fusion.3), channel_id=1, replica_groups=mesh['tiles'=64,'probes'=4] {'tiles'}, use_global_device_ids=true, to_apply=%region_9.10 | all-reduce | flops 8 | bytes 64 | tf_op jit(solution)/shard_map/psum | solution.py:95
  572.1 6.3 collective-permute-start.13
  579.7 10.8 gather_fusion.4
  592.0 4.5 fusion
  596.5 4.1 copy.205
  600.5 5.3 reshape.195
  605.8 23.2 %scatter_custom_fusion.4 = f32[4608,24]{1,0:T(8,128)S(1)} fusion(s32[4096]{0:T(1024)S(1)} %reshape.161, f32[4096,24]{1,0:T(8,128)} %reshape.195, f32[]{:T(128)} %constant.39.clone.1), kind=kCustom, calls=%fused_computation.21 | custom fusion | flops 98304 | bytes 442880 | tf_op jit(solution)/shard_map/scatter-add | solution.py:53
  634.4 5.4 collective-permute-done.14
  641.0 4.0 collective-permute-start.15
  647.2 14.9 %gather_fusion.5 = bf16[4096,24]{1,0:T(8,128)(2,1)} fusion(bf16[4608,24]{1,0:T(8,128)(2,1)S(1)} %copy.208, s32[4096]{0:T(1024)S(1)} %broadcast_clamp_fusion), kind=kCustom, calls=%fused_computation.5 | custom fusion | bytes 409600 | tf_op jit(solution)/shard_map/gather | solution.py:68
  662.1 3.7 reshape.109
  665.8 4.6 convolution_bitcast_fusion
  672.8 22.4 %scatter_custom_fusion.5 = f32[384,8]{1,0:T(8,128)S(1)} fusion(s32[4096]{0:T(1024)S(1)} %reshape.169, f32[4096,8]{1,0:T(8,128)S(1)} %copy.212, f32[]{:T(128)} %constant.39.clone.1), kind=kCustom, calls=%fused_computation.59 | custom fusion | flops 32768 | bytes 12292 | tf_op jit(solution)/shard_map/scatter-add | solution.py:77
  695.4 6.1 collective-permute-start.17
  703.5 5.6 collective-permute-done.16
  709.1 6.7 all_gather.3
  716.8 535.4 %all-reduce.8.cloned.1.call-done = f32[64,8,32]{0,2,1:T(8,128)} async-done(((f32[64,8,32]{0,2,1:T(8,128)}), f32[64,8,32]{0,2,1:T(8,128)}) %all-reduce.8.cloned.1.call-update) | async-done | bytes 65552 | tf_op jit(solution)/shard_map/psum | solution.py:112
  (137 shorter events, 56.9 us)
Async XLA Ops:
  7.2 1245.0 %all-reduce.8.cloned.1.call-start = ((), (), s32[]{:S(2)}) async-start(), calls=%async_computation | async-start | bytes 262144 | tf_op jit(solution)/shard_map/psum | solution.py:112
  8.8 13.1 %collective-permute-start = (f32[64,8]{0,1:T(8,128)S(1)}, f32[64,8]{0,1:T(8,128)S(1)}, u32[]{:S(2)}, u32[]{:S(2)}) collective-permute-start(f32[64,8]{0,1:T(8,128)S(1)} %get-tuple-element.33), channel_id=1, source_target_pairs={{0,4},{4,8},{8,12},{12,16},{16,20},{20,24},{24,28},{28,32},{32,36}... | collective-permute-start | bytes 6152 | tf_op jit(solution)/shard_map/ppermute | solution.py:18
  12.6 9.2 collective-permute-start.1
  48.1 25.2 %copy-start.1 = (s32[64,64]{1,0:T(8,128)S(1)}, s32[64,64]{1,0:T(8,128)}, u32[]{:S(2)}) copy-start(s32[64,64]{1,0:T(8,128)} %param.9) | copy-start | bytes 49156
  48.1 25.2 %copy-start = (f32[4096,3]{0,1:T(4,128)S(1)}, f32[4096,3]{0,1:T(4,128)}, u32[]{:S(2)}) copy-start(f32[4096,3]{0,1:T(4,128)} %param.13) | copy-start | bytes 147460
  71.4 11.9 collective-permute-start.2
  74.8 11.6 copy-start.2
  84.4 5.7 collective-permute-start.3
  138.8 6.1 collective-permute-start.5
  142.9 7.6 collective-permute-start.4
  150.7 157.0 %copy-start.4 = (f32[256,8]{0,1:T(8,128)}, f32[256,8]{0,1:T(8,128)S(1)}, u32[]{:S(2)}) copy-start(f32[256,8]{0,1:T(8,128)S(1)} %get-tuple-element.35) | copy-start | bytes 24580
  287.4 8.1 collective-permute-start.6
  289.3 7.3 collective-permute-start.7
  346.3 10.7 collective-permute-start.8
  358.2 5.7 collective-permute-start.9
  412.6 8.1 collective-permute-start.11
  418.6 7.6 collective-permute-start.10
  570.2 8.2 collective-permute-start.12
  572.1 7.3 collective-permute-start.13
  629.1 10.7 collective-permute-start.14
  641.0 5.7 collective-permute-start.15
  671.9 43.9 %copy-start.5 = (s32[256]{0:T(256)S(1)}, s32[256]{0:T(256)}, u32[]{:S(2)}) copy-start(s32[256]{0:T(256)} %param.15) | copy-start | bytes 3076
  695.4 8.1 collective-permute-start.17
  701.5 7.6 collective-permute-start.16
  709.1 544.6 %copy-start.3 = (f32[256,8]{0,1:T(8,128)}, f32[256,8]{0,1:T(8,128)S(1)}, u32[]{:S(2)}) copy-start(f32[256,8]{0,1:T(8,128)S(1)} %compare_select_fusion.2) | copy-start | bytes 24580
Sparse Core Ops, SparseCore 0:
  716.9 535.2 all-reduce.7
where the time goes:
time: 1270 us; the launch traced here: 1260 us
  waiting for transfers between devices  579 us (46%)
  blocking collectives  287 us (23%)
  other arithmetic  144 us (11%)
  local copies, waits for them, and re-layouts  144 us (11%)
  starting transfers between devices  63.5 us (5%)
  matrix products  28.1 us (2%)
  between operations  15.4 us (1%)
    psum x1, waiting for transfers between devices, shards(): gram = lax.psum(partial_gram, 'tiles')  535 us
    psum x2, blocking collectives, shards(): squares = lax.psum(jnp.sum(current * current, axis=0), 'tiles')  280 us
    scatter-add x3, other arithmetic, hessian(): jax.ops.segment_sum(forward.reshape(elem_slots * node_slots, 3 * group_si...  69.7 us
    scatter-add x3, other arithmetic, hessian(): jax.ops.segment_sum(partials.reshape(elem_slots * node_slots, group_size)...  67.2 us
    gather x3, local copies, waits for them, and re-layouts, hessian(): node_window[connectivity].reshape(elem_slots, block_order, group_size)  44.7 us
    ppermute x12, waiting for transfers between devices, from_behind(): return lax.ppermute(block, axis, route)  41.2 us
    ppermute x12, starting transfers between devices, from_behind(): return lax.ppermute(block, axis, route)  37.5 us
    gather x6, local copies, waits for them, and re-layouts, hessian(): picked = window[basal_map]  35.6 us
  transfers between devices with their start and end apart: 19, of which 12 were waited for; matrix products, arithmetic and copies ran while one was open for 1% of the time, Pallas kernels for 0%

commit v1 on v0

v1 whole, which is shorter than its diff:
```python
import functools

import jax
import jax.numpy as jnp
from jax import lax
from jax.experimental import pallas as pl
from jax.experimental.pallas import tpu as pltpu
from jax.sharding import PartitionSpec as P

F32 = jnp.float32
BF16 = jnp.bfloat16
I32 = jnp.int32
POWER = 2
ROUNDS = POWER + 1
RIM = 64
ELEMS = 64
DOF = 192
PAIRS = 32
CHUNKS = 16
ZS = 8
YXS = 8
GROUPS = 4
EDGE = (0, 1, 16, 17)
INNER = tuple(range(2, 16))
NT = (((1,), (1,)), ((), ()))
NN = (((1,), (0,)), ((), ()))
MESH = pl.DeviceIdType.MESH


def mo(x, n):
    return pl.multiple_of(x, n)


def split(x):
    hi = x.astype(BF16).astype(F32)
    return hi, x - hi


def dot(a, b, dims=NN):
    return lax.dot_general(a, b, dims, preferred_element_type=F32)


def kernel(
    blk_hbm, idx_ref, fr_ref, w_ref, qs_ref, cl_ref,
    samp_ref, refd_ref, gram_ref,
    blk, ohn, ohnt, ohc, ohct, an8, ac8, fr8, rep, sel, pm, pmt,
    gh, gl, xin, fw, fc, acce, acci, te, ti, ad1, ad, ain, yh, yl, pt,
    wn, qsp, qsn, renext, reprev, bs, rbn, rbp, pa, pb, cp, gk, ka, kb, kc,
    blk_sem, i_s, i_r, e_s, e_r, b_s, b_r, p_s, p_r, g_s, g_r, k_s, k_r,
):
    tile = lax.axis_index("tiles")
    group = lax.axis_index("probes")
    tiles = lax.axis_size("tiles")
    nxt = lax.rem(tile + 1, tiles)
    prv = lax.rem(tile + tiles - 1, tiles)
    my_z = lax.rem(tile, ZS)
    my_yx = lax.div(tile, ZS)
    has_prev = jnp.where(tile > 0, 1.0, 0.0).astype(F32)
    has_next = jnp.where(tile < tiles - 1, 1.0, 0.0).astype(F32)

    def z_peer(d):
        return lax.rem(my_z + d, ZS)

    def yx_peer(d):
        return lax.rem(my_yx + d, YXS)

    def z_device(z):
        return (my_yx * ZS + z, group)

    def yx_device(yx):
        return (yx * ZS + my_z, group)

    def rcopy(src, dst, ss, rs, dev):
        return pltpu.make_async_remote_copy(
            src_ref=src, dst_ref=dst, send_sem=ss, recv_sem=rs, device_id=dev, device_id_type=MESH
        )

    load = pltpu.make_async_copy(blk_hbm, blk, blk_sem)
    load.start()

    barrier = pltpu.get_barrier_semaphore()

    def greet(dev):
        pl.semaphore_signal(barrier, inc=1, device_id=dev, device_id_type=MESH)

    greet((nxt, group))
    greet((prv, group))
    for d in range(1, ZS):
        greet(z_device(z_peer(d)))
    for d in range(1, YXS):
        greet(yx_device(yx_peer(d)))
    for d in range(1, GROUPS):
        greet((tile, lax.rem(group + d, GROUPS)))

    def one(cond):
        return jnp.where(cond, 1.0, 0.0).astype(BF16)

    def pair_col(lane):
        half = lane >> 8
        j = lane & 255
        k = (j * 171) >> 9
        return half, k, j - 3 * k, j < DOF

    r = lax.broadcasted_iota(I32, (128, 512), 0)
    half, k, c, ok = pair_col(lax.broadcasted_iota(I32, (128, 512), 1))
    rep[...] = one((r == half * 64 + k) & ok)
    half, k, c, ok = pair_col(lax.broadcasted_iota(I32, (512, 128), 0))
    r = lax.broadcasted_iota(I32, (512, 128), 1)
    sel[...] = one((r == half * 64 + k) & ok)
    r = lax.broadcasted_iota(I32, (384, 512), 0)
    half, k, c, ok = pair_col(lax.broadcasted_iota(I32, (384, 512), 1))
    pm[...] = one((r == c * 128 + half * 64 + k) & ok)
    half, k, c, ok = pair_col(lax.broadcasted_iota(I32, (512, 384), 0))
    r = lax.broadcasted_iota(I32, (512, 384), 1)
    pmt[...] = one((r == c * 128 + half * 64 + k) & ok)

    fw[...] = jnp.zeros(fw.shape, BF16)
    yh[...] = jnp.zeros(yh.shape, BF16)
    yl[...] = jnp.zeros(yl.shape, BF16)

    for i in range(PAIRS):
        rows = slice(i * 8, i * 8 + 8)
        fr8[rows, :] = jnp.broadcast_to(fr_ref[i : i + 1, :], (8, 512))
    for i in range(CHUNKS):
        rows = slice(i * 8, i * 8 + 8)
        for j in range(2):
            lanes = slice(j * 128, j * 128 + 128)
            n = 2 * i + j
            an8[rows, lanes] = jnp.broadcast_to(idx_ref[n : n + 1, :] >> 8, (8, 128))
            ac8[rows, lanes] = jnp.broadcast_to(idx_ref[PAIRS + n : PAIRS + n + 1, :] >> 7, (8, 128))

    low = jnp.where(
        lax.broadcasted_iota(I32, (64, 128), 0) < PAIRS, idx_ref[...] & 255, idx_ref[...] & 127
    ).astype(F32)
    cols = jnp.transpose(jnp.concatenate([low, jnp.zeros((64, 128), F32)], axis=0))
    sub_n = lax.broadcasted_iota(I32, (256, 128), 0)
    sub_c = lax.broadcasted_iota(I32, (128, 128), 0)
    lane_n = lax.broadcasted_iota(I32, (128, 256), 1).astype(F32)
    lane_c = lax.broadcasted_iota(I32, (128, 128), 1).astype(F32)
    for i in range(PAIRS):
        span = slice(i * 128, i * 128 + 128)
        ohn[:, span] = one(sub_n == (idx_ref[i : i + 1, :] & 255))
        ohc[:, span] = one(sub_c == (idx_ref[PAIRS + i : PAIRS + i + 1, :] & 127))
        ohnt[span, :] = one(lane_n == cols[:, i : i + 1])
        ohct[span, :] = one(lane_c == cols[:, PAIRS + i : PAIRS + i + 1])

    pl.semaphore_wait(barrier, 2 + ZS - 1 + YXS - 1 + GROUPS - 1)

    first = [
        rcopy(qs_ref.at[:, pl.ds(256, 128)], qsp, i_s.at[0], i_r.at[0], (nxt, group)),
        rcopy(qs_ref.at[:, pl.ds(0, 128)], qsn, i_s.at[1], i_r.at[1], (prv, group)),
        rcopy(w_ref.at[pl.ds(0, 8), :], wn, i_s.at[2], i_r.at[2], (prv, group)),
    ]
    for cpy in first:
        cpy.start()
    for cpy in first:
        cpy.wait()
    load.wait()

    lane = lax.broadcasted_iota(I32, (8, 128), 1)
    upper = jnp.where(lane >= RIM, 1.0, 0.0).astype(F32)
    own = [upper, jnp.ones((8, 128), F32), 1.0 - upper]
    exist = [
        upper + (1.0 - upper) * has_prev,
        jnp.ones((8, 128), F32),
        (1.0 - upper) + upper * has_next,
    ]
    q = [
        qs_ref[0:8, 0:128] + qsp[0:8, :] * has_prev,
        qs_ref[0:8, 128:256],
        qs_ref[0:8, 256:384] + qsn[0:8, :] * has_next,
    ]
    same = [
        qs_ref[8:16, 0:128] + qsp[8:16, :] * has_prev,
        qs_ref[8:16, 128:256],
        qs_ref[8:16, 256:384] + qsn[8:16, :] * has_next,
    ]

    def square_start(i, cur):
        total = cur[0] * cur[0] * own[0] + cur[1] * cur[1] + cur[2] * cur[2] * own[2]
        pa[i, my_z] = total
        for d in range(1, ZS):
            rcopy(
                pa.at[i, my_z], pa.at[i, my_z], p_s.at[i, 0, d], p_r.at[i, 0, my_z],
                z_device(z_peer(d)),
            ).start()

    def square_mid(i):
        for d in range(1, ZS):
            z = z_peer(d)
            got = rcopy(pa.at[i, z], pa.at[i, z], p_s.at[i, 0, d], p_r.at[i, 0, z], z_device(z))
            got.wait_recv()
            got.wait_send()
        total = pa[i, 0]
        for z in range(1, ZS):
            total = total + pa[i, z]
        pb[i, my_yx] = total
        for d in range(1, YXS):
            rcopy(
                pb.at[i, my_yx], pb.at[i, my_yx], p_s.at[i, 1, d], p_r.at[i, 1, my_yx],
                yx_device(yx_peer(d)),
            ).start()

    def square_end(i):
        for d in range(1, YXS):
            yx = yx_peer(d)
            got = rcopy(
                pb.at[i, yx], pb.at[i, yx], p_s.at[i, 1, d], p_r.at[i, 1, yx], yx_device(yx)
            )
            got.wait_recv()
            got.wait_send()
        total = pb[i, 0]
        for yx in range(1, YXS):
            total = total + pb[i, yx]
        mean = jnp.sum(total, axis=1, keepdims=True) / (256 * tiles)
        return 1.0 / jnp.sqrt(mean + 1e-06)

    row16 = lax.broadcasted_iota(I32, (16, DOF), 0) < 8

    def scatter_nodes(m, levels):
        r0 = mo(m * 16, 16)
        parts = []
        for c in range(3):
            span = slice(c * 128, c * 128 + 128)
            parts.append(
                jnp.concatenate([fc[pl.ds(r0, 8), span], fc[pl.ds(r0 + 8, 8), span]], axis=1)
            )
        a = an8[pl.ds(mo(m * 8, 8), 8), :]
        spread = jnp.concatenate(
            [jnp.where(a == lv, parts[c], 0.0) for lv in levels for c in range(3)], axis=0
        )
        return dot(spread.astype(BF16), ohnt[pl.ds(mo(m * 256, 256), 256), :])

    def gather_nodes(m, table, levels, base):
        got = dot(table[...], ohn[:, pl.ds(mo(m * 256, 256), 256)])
        a = an8[pl.ds(mo(m * 8, 8), 8), :]
        out = list(base)
        for n, lv in enumerate(levels):
            hit = a == lv
            for c in range(3):
                row = (n * 3 + c) * 8
                out[c] = jnp.where(hit, got[row : row + 8], out[c])
        return out

    def hessian(h, q):
        parts = []
        for b in q:
            parts += list(split(b))
        cells = jnp.concatenate(parts, axis=0).astype(BF16)

        @pl.loop(0, CHUNKS)
        def _(m):
            got = dot(cells, ohc[:, pl.ds(mo(m * 256, 256), 256)])
            a = ac8[pl.ds(mo(m * 8, 8), 8), :]
            g = jnp.where(
                a == 0,
                got[0:8] + got[8:16],
                jnp.where(a == 1, got[16:24] + got[24:32], got[32:40] + got[40:48]),
            )
            hi, lo = split(g)
            rows = pl.ds(mo(m * 16, 16), 16)
            gh[rows, :] = jnp.concatenate([hi[:, :128], hi[:, 128:]], axis=0).astype(BF16)
            gl[rows, :] = jnp.concatenate([lo[:, :128], lo[:, 128:]], axis=0).astype(BF16)

        for i in range(4):
            rows = slice(i * 64, i * 64 + 64)
            wide = dot(gh[rows, :], rep[...]) + dot(gl[rows, :], rep[...])
            xin[rows, :] = (wide * fr8[rows, :]).astype(BF16)

        @pl.loop(0, CHUNKS)
        def _(m):
            rows = pl.ds(mo(m * 16, 16), 16)
            for half in range(2):
                span = slice(half * 256, half * 256 + DOF)
                x = xin[rows, span]
                o0 = dot(x, blk[4 * m + half], NT)
                o1 = dot(x, blk[4 * m + 2 + half], NT)
                fw[rows, span] = jnp.where(row16, o0, o1).astype(BF16)

        for i in range(4):
            rows = slice(i * 64, i * 64 + 64)
            fc[rows, :] = dot(fw[rows, :], pmt[...])

        acce[...] = jnp.zeros(acce.shape, F32)
        acci[...] = jnp.zeros(acci.shape, F32)

        @pl.loop(0, CHUNKS)
        def _(m):
            acce[...] += scatter_nodes(m, EDGE)

        swap = [
            rcopy(acce.at[pl.ds(0, 48), :], renext.at[h], e_s.at[h, 0], e_r.at[h, 0], (prv, group)),
            rcopy(acce.at[pl.ds(48, 48), :], reprev.at[h], e_s.at[h, 1], e_r.at[h, 1], (nxt, group)),
        ]
        for cpy in swap:
            cpy.start()

        @pl.loop(0, CHUNKS)
        def _(m):
            acci[...] += scatter_nodes(m, INNER)

        if h > 0:
            square_mid(h - 1)

        for i in range(21):
            pair = []
            for j in range(2):
                n = 2 * i + j
                pair.append(acci[n * 8 : n * 8 + 8, :] * w_ref[6 + n : 7 + n, :])
            ti[i * 16 : i * 16 + 16, :] = jnp.concatenate(pair, axis=0).astype(BF16)

        @pl.loop(0, CHUNKS)
        def _(m):
            zero = jnp.zeros((8, 256), F32)
            out = gather_nodes(m, ti, INNER, [zero] * 3)
            r0 = mo(m * 16, 16)
            for c in range(3):
                span = slice(c * 128, c * 128 + 128)
                ad1[pl.ds(r0, 8), span] = out[c][:, :128]
                ad1[pl.ds(r0 + 8, 8), span] = out[c][:, 128:]

        for cpy in swap:
            cpy.wait()
        for i in range(6):
            pair = []
            for j in range(2):
                n = 2 * i + j
                if n < 6:
                    total = acce[n * 8 : n * 8 + 8, :] + reprev[h, n * 8 : n * 8 + 8, :] * has_prev
                    pair.append(total * w_ref[n : n + 1, :])
                else:
                    o = (n - 6) * 8
                    total = acce[n * 8 : n * 8 + 8, :] + renext[h, o : o + 8, :]
                    pair.append(total * (wn[n - 6 : n - 5, :] * has_next))
            te[i * 16 : i * 16 + 16, :] = jnp.concatenate(pair, axis=0).astype(BF16)

        @pl.loop(0, CHUNKS)
        def _(m):
            r0 = mo(m * 16, 16)
            base = []
            for c in range(3):
                span = slice(c * 128, c * 128 + 128)
                base.append(
                    jnp.concatenate([ad1[pl.ds(r0, 8), span], ad1[pl.ds(r0 + 8, 8), span]], axis=1)
                )
            out = gather_nodes(m, te, EDGE, base)
            for c in range(3):
                span = slice(c * 128, c * 128 + 128)
                ad[pl.ds(r0, 16), span] = jnp.concatenate(
                    [out[c][:, :128], out[c][:, 128:]], axis=0
                ).astype(BF16)

        for i in range(4):
            rows = slice(i * 64, i * 64 + 64)
            ain[rows, :] = dot(ad[rows, :], pm[...]).astype(BF16)

        @pl.loop(0, CHUNKS)
        def _(m):
            rows = pl.ds(mo(m * 16, 16), 16)
            for half in range(2):
                span = slice(half * 256, half * 256 + DOF)
                x = ain[rows, span]
                o0 = dot(x, blk[4 * m + half])
                o1 = dot(x, blk[4 * m + 2 + half])
                hi, lo = split(jnp.where(row16, o0, o1) * fr8[rows, span])
                yh[rows, span] = hi.astype(BF16)
                yl[rows, span] = lo.astype(BF16)

        for i in range(4):
            rows = slice(i * 64, i * 64 + 64)
            pt[rows, :] = dot(yh[rows, :], sel[...]) + dot(yl[rows, :], sel[...])

        def scatter_cells(m, acc):
            r0 = mo(m * 16, 16)
            v = jnp.concatenate([pt[pl.ds(r0, 8), :], pt[pl.ds(r0 + 8, 8), :]], axis=1)
            a = ac8[pl.ds(mo(m * 8, 8), 8), :]
            spread = jnp.concatenate(
                [jnp.where(a == lv, s, 0.0) for lv in range(3) for s in split(v)], axis=0
            )
            return acc + dot(spread.astype(BF16), ohct[pl.ds(mo(m * 256, 256), 256), :])

        acc = lax.fori_loop(0, CHUNKS, scatter_cells, jnp.zeros((48, 128), F32))
        sums = [acc[n * 16 : n * 16 + 8] + acc[n * 16 + 8 : n * 16 + 16] for n in range(3)]
        bs[h, 0] = sums[0]
        bs[h, 1] = sums[2]
        swap = [
            rcopy(bs.at[h, 0], rbn.at[h], b_s.at[h, 0], b_r.at[h, 0], (prv, group)),
            rcopy(bs.at[h, 1], rbp.at[h], b_s.at[h, 1], b_r.at[h, 1], (nxt, group)),
        ]
        for cpy in swap:
            cpy.start()
        scale = square_end(h - 1) if h > 0 else None
        for cpy in swap:
            cpy.wait()
        sums[0] = sums[0] + rbp[h] * has_prev
        sums[2] = sums[2] + rbn[h] * has_next
        keep = same if h % 2 == 1 else [exist[n] - same[n] for n in range(3)]
        out = []
        for n in range(3):
            v = sums[n] * keep[n]
            out.append(v if scale is None else v * scale)
        return out

    for h in range(ROUNDS):
        q = hessian(h, q)
        if h < POWER:
            square_start(h, q)
        if h == 0:
            for n in range(3):
                samp_ref[:, n * 128 : n * 128 + 128] = q[n]
    for n in range(3):
        refd_ref[:, n * 128 : n * 128 + 128] = q[n]

    mine = pltpu.roll(refd_ref[...], 384 - RIM, 1)[:, :256]
    cp[group] = mine
    for d in range(1, GROUPS):
        rcopy(
            cp.at[group], cp.at[group], g_s.at[d], g_r.at[group], (tile, lax.rem(group + d, GROUPS))
        ).start()
    for d in range(1, GROUPS):
        g = lax.rem(group + d, GROUPS)
        got = rcopy(cp.at[g], cp.at[g], g_s.at[d], g_r.at[g], (tile, g))
        got.wait_recv()
        got.wait_send()
    every = jnp.concatenate([cp[g] for g in range(GROUPS)], axis=0)
    outer = jnp.concatenate([every * mine[i : i + 1, :] for i in range(8)], axis=0)
    hi, lo = split(outer)
    member = one(lax.broadcasted_iota(I32, (64, 256), 0) == cl_ref[...])
    gk[...] = dot(member, hi.astype(BF16), NT) + dot(member, lo.astype(BF16), NT)

    ka[my_z] = gk[pl.ds(mo(my_z * 8, 8), 8), :]
    for d in range(1, ZS):
        z = z_peer(d)
        rcopy(
            gk.at[pl.ds(mo(z * 8, 8), 8), :], ka.at[my_z], k_s.at[0, d], k_r.at[0, my_z],
            z_device(z),
        ).start()
    for d in range(1, ZS):
        z = z_peer(d)
        got = rcopy(ka.at[z], ka.at[z], k_s.at[0, d], k_r.at[0, z], z_device(z))
        got.wait_recv()
        got.wait_send()
    total = ka[0]
    for z in range(1, ZS):
        total = total + ka[z]
    kb[my_yx] = total
    for d in range(1, YXS):
        rcopy(
            kb.at[my_yx], kb.at[my_yx], k_s.at[1, d], k_r.at[1, my_yx], yx_device(yx_peer(d))
        ).start()
    for d in range(1, YXS):
        yx = yx_peer(d)
        got = rcopy(kb.at[yx], kb.at[yx], k_s.at[1, d], k_r.at[1, yx], yx_device(yx))
        got.wait_recv()
        got.wait_send()
    total = kb[0]
    for yx in range(1, YXS):
        total = total + kb[yx]
    kc[my_z] = total
    for d in range(1, ZS):
        rcopy(
            kc.at[my_z], kc.at[my_z], k_s.at[2, d], k_r.at[2, my_z], z_device(z_peer(d))
        ).start()
    for d in range(1, ZS):
        z = z_peer(d)
        got = rcopy(kc.at[z], kc.at[z], k_s.at[2, d], k_r.at[2, z], z_device(z))
        got.wait_recv()
        got.wait_send()
    for z in range(ZS):
        gram_ref[z * 8 : z * 8 + 8, :] = kc[z]


def shards(
    blocks, connectivity, basal_map, friction, elem_counts, obs_weight, sign_bits, cluster_ids
):
    live = jnp.arange(ELEMS, dtype=I32) < elem_counts[0]
    fr = jnp.where(live[:, None], friction.reshape(ELEMS, DOF), 0.0)
    fr = jnp.pad(fr, ((0, 0), (0, 256 - DOF))).reshape(PAIRS, 512)
    idx = jnp.concatenate([connectivity.reshape(PAIRS, 128), basal_map.reshape(PAIRS, 128)], axis=0)
    w = obs_weight.reshape(16, 256, 3).transpose(0, 2, 1).reshape(48, 256)
    parity = jnp.arange(8, dtype=I32)[:, None] % 2
    same = (cluster_ids % 2)[None, :] == parity
    start = jnp.where(same, (2 * sign_bits.T - 1).astype(F32), 0.0)
    qs = jnp.pad(jnp.concatenate([start, same.astype(F32)], axis=0), ((0, 0), (RIM, RIM)))
    cl = cluster_ids.reshape(1, 256)

    vmem = pl.BlockSpec(memory_space=pltpu.VMEM)
    dma = pltpu.SemaphoreType.DMA
    samp, refd, gram = pl.pallas_call(
        kernel,
        out_shape=(
            jax.ShapeDtypeStruct((8, 384), F32),
            jax.ShapeDtypeStruct((8, 384), F32),
            jax.ShapeDtypeStruct((64, 256), F32),
        ),
        in_specs=[pl.BlockSpec(memory_space=pl.ANY)] + [vmem] * 5,
        out_specs=(vmem, vmem, vmem),
        scratch_shapes=[
            pltpu.VMEM((ELEMS, DOF, DOF), BF16),
            pltpu.VMEM((256, 4096), BF16),
            pltpu.VMEM((4096, 256), BF16),
            pltpu.VMEM((128, 4096), BF16),
            pltpu.VMEM((4096, 128), BF16),
            pltpu.VMEM((128, 256), I32),
            pltpu.VMEM((128, 256), I32),
            pltpu.VMEM((256, 512), F32),
            pltpu.VMEM((128, 512), BF16),
            pltpu.VMEM((512, 128), BF16),
            pltpu.VMEM((384, 512), BF16),
            pltpu.VMEM((512, 384), BF16),
            pltpu.VMEM((256, 128), BF16),
            pltpu.VMEM((256, 128), BF16),
            pltpu.VMEM((256, 512), BF16),
            pltpu.VMEM((256, 512), BF16),
            pltpu.VMEM((256, 384), F32),
            pltpu.VMEM((96, 256), F32),
            pltpu.VMEM((336, 256), F32),
            pltpu.VMEM((96, 256), BF16),
            pltpu.VMEM((336, 256), BF16),
            pltpu.VMEM((256, 384), F32),
            pltpu.VMEM((256, 384), BF16),
            pltpu.VMEM((256, 512), BF16),
            pltpu.VMEM((256, 512), BF16),
            pltpu.VMEM((256, 512), BF16),
            pltpu.VMEM((256, 128), F32),
            pltpu.VMEM((8, 256), F32),
            pltpu.VMEM((16, 128), F32),
            pltpu.VMEM((16, 128), F32),
            pltpu.VMEM((ROUNDS, 48, 256), F32),
            pltpu.VMEM((ROUNDS, 48, 256), F32),
            pltpu.VMEM((ROUNDS, 2, 8, 128), F32),
            pltpu.VMEM((ROUNDS, 8, 128), F32),
            pltpu.VMEM((ROUNDS, 8, 128), F32),
            pltpu.VMEM((POWER, ZS, 8, 128), F32),
            pltpu.VMEM((POWER, YXS, 8, 128), F32),
            pltpu.VMEM((GROUPS, 8, 256), F32),
            pltpu.VMEM((64, 256), F32),
            pltpu.VMEM((ZS, 8, 256), F32),
            pltpu.VMEM((YXS, 8, 256), F32),
            pltpu.VMEM((ZS, 8, 256), F32),
            dma,
            dma((3,)),
            dma((3,)),
            dma((ROUNDS, 2)),
            dma((ROUNDS, 2)),
            dma((ROUNDS, 2)),
            dma((ROUNDS, 2)),
            dma((POWER, 2, 8)),
            dma((POWER, 2, 8)),
            dma((GROUPS,)),
            dma((GROUPS,)),
            dma((3, 8)),
            dma((3, 8)),
        ],
        compiler_params=pltpu.CompilerParams(
            collective_id=0, has_side_effects=True, vmem_limit_bytes=48 * 1024 * 1024
        ),
    )(blocks, idx, fr, w, qs, cl)
    samples = samp[:, RIM : RIM + 256].T
    refined = refd[:, RIM : RIM + 256].T
    return samples, refined, gram.reshape(64, 8, 32)


def solution(mesh):
    in_specs = (
        P("tiles", None, None),
        P("tiles", None),
        P("tiles", None),
        P("tiles", None, None),
        P("tiles"),
        P("tiles", None),
        P("tiles", "probes"),
        P("tiles"),
    )
    out_specs = (P("tiles", "probes"), P("tiles", "probes"), P(None, "probes", None))
    return jax.shard_map(shards, mesh=mesh, in_specs=in_specs, out_specs=out_specs, check_vma=False)
```

time: 1270 us -> 129 us (0.10)
  waiting for transfers between devices: 579 us -> 0 us
  blocking collectives: 287 us -> 0 us
  other arithmetic: 144 us -> 1.63 us
  local copies, waits for them, and re-layouts: 144 us -> 5.78 us
  Pallas kernels: 0 us -> 119 us
  starting transfers between devices: 63.5 us -> 0 us
  matrix products: 28.1 us -> 0 us
  between operations: 15.4 us -> 1.36 us
    psum x1 -> x0, waiting for transfers between devices: 535 us -> none  [shards(): gram = lax.psum(partial_gram, 'tiles')]
    psum x2 -> x0, blocking collectives: 280 us -> none  [shards(): squares = lax.psum(jnp.sum(current * current, axis=0), 'tiles')]
    scatter-add x6 -> x0, other arithmetic: 137 us -> none  [the longest x3 69.7 us: hessian(): jax.ops.segment_sum(forward.reshape(elem_slots * node_slots, 3 * group_si...]
    pallas_call x0 -> x1, Pallas kernels: none -> 119 us  [shards(): pl.pallas_call(kernel, out_shape=(jax.ShapeDtypeStruct((8, 384), F32), ja...]
    gather x9 -> x0, local copies, waits for them, and re-layouts: 80.3 us -> none  [the longest x3 44.7 us: hessian(): node_window[connectivity].reshape(elem_slots, block_order, group_size)]
    ppermute x18 -> x0, starting transfers between devices: 63.4 us -> none  [the longest x12 37.5 us: from_behind(): return lax.ppermute(block, axis, route)]
    ppermute x18 -> x0, waiting for transfers between devices: 43.4 us -> none  [the longest x12 41.2 us: from_behind(): return lax.ppermute(block, axis, route)]
    dot_general x7 -> x0, matrix products: 28.1 us -> none  [the longest x3 13.7 us: hessian(): jnp.einsum('eji,ejp->eip', blocks, adjoint_in, preferred_element_type=jnp...]
  transfers between devices with their start and end apart: 19 -> 0, of which waited for: 12 -> 0; matrix products, arithmetic and copies ran while one was open for 1% -> 0% of each run, Pallas kernels for 0% -> 0%
where the time goes in v1:
time: 129 us; the launch traced here: 128 us
  Pallas kernels  119 us (92%)
  local copies, waits for them, and re-layouts  5.78 us (4%)
  other arithmetic  1.63 us (1%)
  between operations  1.36 us (1%)
    pallas_call x1, Pallas kernels, shards(): pl.pallas_call(kernel, out_shape=(jax.ShapeDtypeStruct((8, 384), F32), ja...  119 us

profile of v1, /device:TPU:2, one launch (start us, length us, event | category | flops | bytes accessed | tf_op | source)
XLA Modules:
  0.0 127.9 jit_solution(850245928836611733)
XLA Ops:
  0.6 0.7 and_select_fusion.1
  1.3 0.1 compare_convert_fusion
  1.4 0.8 compare_select_fusion
  2.2 0.1 select_maximum_fusion.qs_ref
  2.2 1.0 copy.13
  4.0 0.1 copy.17
  4.1 0.8 reshape.50
  4.9 0.8 reshape.51
  5.8 0.9 reshape.55.w_ref
  6.6 0.0 copy-start
  6.7 0.7 copy-done
  7.3 119.1 %shard_map.103 = (f32[8,384]{1,0:T(8,128)S(1)}, f32[8,384]{1,0:T(8,128)S(1)}, f32[64,256]{1,0:T(8,128)S(1)}) custom-call(bf16[64,192,192]{2,1,0:T(8,128)(2,1)} %blk_hbm.1, s32[64,128]{1,0:T(8,128)S(1)} %pad_add_fusion.idx_ref, f32[32,512]{1,0:T(8,128)S(1)} %reshape.53.fr_ref, f32[48,256]{1,0:T(8,128)S(1)} %reshape.55.w_ref, ...), custom_call_target="tpu_custom_call" | custom-call | tf_op jit(solution)/shard_map/pallas_call | solution.py:489
  126.5 0.7 slice_bitcast_fusion
  127.2 0.8 copy.16
  (7 shorter events, 0.1 us)
Async XLA Ops:
  6.6 0.7 copy-start

commit v2 on v1

--- a/solution.py
+++ b/solution.py
@@ -17,6 +17,12 @@
 DOF = 192
 PAIRS = 32
 CHUNKS = 16
+U_IN = 16
+U_PROD = 16
+U_EDGE = 16
+U_INNER = 16
+U_GET = 16
+U_PUT = 16
 ZS = 8
 YXS = 8
 GROUPS = 4
@@ -31,6 +37,13 @@
     return pl.multiple_of(x, n)
 
 
+def each(unroll, body):
+    @pl.loop(0, CHUNKS // unroll)
+    def _(n):
+        for j in range(unroll):
+            body(n * unroll + j)
+
+
 def split(x):
     hi = x.astype(BF16).astype(F32)
     return hi, x - hi
@@ -41,12 +54,13 @@
 
 
 def kernel(
-    blk_hbm, idx_ref, fr_ref, w_ref, qs_ref, cl_ref,
+    blk_hbm, conn_hbm, cell_hbm, fr_hbm, count_ref, w_hbm, sign_hbm, cl_hbm,
     samp_ref, refd_ref, gram_ref,
+    conn, cell, fr3, w3, sign, cl_ref, idx_ref, qs_ref,
     blk, ohn, ohnt, ohc, ohct, an8, ac8, fr8, rep, sel, pm, pmt,
     gh, gl, xin, fw, fc, acce, acci, te, ti, ad1, ad, ain, yh, yl, pt,
     wn, qsp, qsn, renext, reprev, bs, rbn, rbp, pa, pb, cp, gk, ka, kb, kc,
-    blk_sem, i_s, i_r, e_s, e_r, b_s, b_r, p_s, p_r, g_s, g_r, k_s, k_r,
+    blk_sem, in_sem, i_s, i_r, e_s, e_r, b_s, b_r, p_s, p_r, g_s, g_r, k_s, k_r,
 ):
     tile = lax.axis_index("tiles")
     group = lax.axis_index("probes")
@@ -75,6 +89,14 @@
             src_ref=src, dst_ref=dst, send_sem=ss, recv_sem=rs, device_id=dev, device_id_type=MESH
         )
 
+    small = [
+        pltpu.make_async_copy(src, dst, in_sem.at[n])
+        for n, (src, dst) in enumerate(
+            [(sign_hbm, sign), (cl_hbm, cl_ref), (w_hbm, w3), (conn_hbm, conn), (cell_hbm, cell), (fr_hbm, fr3)]
+        )
+    ]
+    for cpy in small:
+        cpy.start()
     load = pltpu.make_async_copy(blk_hbm, blk, blk_sem)
     load.start()
 
@@ -118,9 +140,42 @@
     yh[...] = jnp.zeros(yh.shape, BF16)
     yl[...] = jnp.zeros(yl.shape, BF16)
 
+    for cpy in small:
+        cpy.wait()
+
+    same_own = (cl_ref[...] & 1) == (lax.broadcasted_iota(I32, (8, 256), 0) & 1)
+    start = jnp.where(same_own, (2 * sign[...] - 1).astype(F32), 0.0)
+    both = jnp.concatenate([start, jnp.where(same_own, 1.0, 0.0).astype(F32)], axis=0)
+    qs_ref[...] = pltpu.roll(
+        jnp.concatenate([both, jnp.zeros((16, 128), F32)], axis=1), RIM, 1
+    )
+    first = [
+        rcopy(qs_ref.at[:, pl.ds(256, 128)], qsp, i_s.at[0], i_r.at[0], (nxt, group)),
+        rcopy(qs_ref.at[:, pl.ds(0, 128)], qsn, i_s.at[1], i_r.at[1], (prv, group)),
+        rcopy(w3.at[:, pl.ds(0, 512)], wn, i_s.at[2], i_r.at[2], (prv, group)),
+    ]
+    pl.semaphore_wait(barrier, 2 + ZS - 1 + YXS - 1 + GROUPS - 1)
+    for cpy in first:
+        cpy.start()
+
+    idx_ref[0:PAIRS, :] = jnp.concatenate([conn[0:PAIRS, :], conn[PAIRS:ELEMS, :]], axis=1)
+    idx_ref[PAIRS:ELEMS, :] = jnp.concatenate([cell[0:PAIRS, :], cell[PAIRS:ELEMS, :]], axis=1)
+    element = lax.broadcasted_iota(I32, (PAIRS, 128), 0) + jnp.where(
+        lax.broadcasted_iota(I32, (PAIRS, 128), 1) < 64, 0, PAIRS
+    )
+    live = element < count_ref[0]
+    wide = []
+    for c in range(3):
+        f = jnp.concatenate([fr3[c, 0:PAIRS, :], fr3[c, PAIRS:ELEMS, :]], axis=1)
+        wide.append(jnp.where(live, f, 0.0))
+    wide = jnp.concatenate(wide, axis=1)
+    hi, rest = split(wide)
+    mid, lo = split(rest)
+    third = dot(jnp.concatenate([hi, mid, lo], axis=0).astype(BF16), pm[...])
+    fr = third[0:PAIRS] + third[PAIRS : 2 * PAIRS] + third[2 * PAIRS :]
     for i in range(PAIRS):
         rows = slice(i * 8, i * 8 + 8)
-        fr8[rows, :] = jnp.broadcast_to(fr_ref[i : i + 1, :], (8, 512))
+        fr8[rows, :] = jnp.broadcast_to(fr[i : i + 1, :], (8, 512))
     for i in range(CHUNKS):
         rows = slice(i * 8, i * 8 + 8)
         for j in range(2):
@@ -144,15 +199,6 @@
         ohnt[span, :] = one(lane_n == cols[:, i : i + 1])
         ohct[span, :] = one(lane_c == cols[:, PAIRS + i : PAIRS + i + 1])
 
-    pl.semaphore_wait(barrier, 2 + ZS - 1 + YXS - 1 + GROUPS - 1)
-
-    first = [
-        rcopy(qs_ref.at[:, pl.ds(256, 128)], qsp, i_s.at[0], i_r.at[0], (nxt, group)),
-        rcopy(qs_ref.at[:, pl.ds(0, 128)], qsn, i_s.at[1], i_r.at[1], (prv, group)),
-        rcopy(w_ref.at[pl.ds(0, 8), :], wn, i_s.at[2], i_r.at[2], (prv, group)),
-    ]
-    for cpy in first:
-        cpy.start()
     for cpy in first:
         cpy.wait()
     load.wait()
@@ -215,21 +261,30 @@
         mean = jnp.sum(total, axis=1, keepdims=True) / (256 * tiles)
         return 1.0 / jnp.sqrt(mean + 1e-06)
 
+    def weight(ref, n):
+        c = n % 3
+        return ref[c : c + 1, n // 3 * 256 : n // 3 * 256 + 256]
+
     row16 = lax.broadcasted_iota(I32, (16, DOF), 0) < 8
 
-    def scatter_nodes(m, levels):
-        r0 = mo(m * 16, 16)
-        parts = []
-        for c in range(3):
-            span = slice(c * 128, c * 128 + 128)
-            parts.append(
-                jnp.concatenate([fc[pl.ds(r0, 8), span], fc[pl.ds(r0 + 8, 8), span]], axis=1)
+    def scatter_nodes(n, unroll, levels):
+        spreads = []
+        for j in range(unroll):
+            m = n * unroll + j
+            r0 = mo(m * 16, 16)
+            parts = []
+            for c in range(3):
+                span = slice(c * 128, c * 128 + 128)
+                parts.append(
+                    jnp.concatenate([fc[pl.ds(r0, 8), span], fc[pl.ds(r0 + 8, 8), span]], axis=1)
+                )
+            a = an8[pl.ds(mo(m * 8, 8), 8), :]
+            spread = jnp.concatenate(
+                [jnp.where(a == lv, parts[c], 0.0) for lv in levels for c in range(3)], axis=0
             )
-        a = an8[pl.ds(mo(m * 8, 8), 8), :]
-        spread = jnp.concatenate(
-            [jnp.where(a == lv, parts[c], 0.0) for lv in levels for c in range(3)], axis=0
-        )
-        return dot(spread.astype(BF16), ohnt[pl.ds(mo(m * 256, 256), 256), :])
+            spreads.append(spread.astype(BF16))
+        size = unroll * 256
+        return dot(jnp.concatenate(spreads, axis=1), ohnt[pl.ds(mo(n * size, size), size), :])
 
     def gather_nodes(m, table, levels, base):
         got = dot(table[...], ohn[:, pl.ds(mo(m * 256, 256), 256)])
@@ -248,8 +303,7 @@
             parts += list(split(b))
         cells = jnp.concatenate(parts, axis=0).astype(BF16)
 
-        @pl.loop(0, CHUNKS)
-        def _(m):
+        def gather_cells(m):
             got = dot(cells, ohc[:, pl.ds(mo(m * 256, 256), 256)])
             a = ac8[pl.ds(mo(m * 8, 8), 8), :]
             g = jnp.where(
@@ -262,20 +316,23 @@
             gh[rows, :] = jnp.concatenate([hi[:, :128], hi[:, 128:]], axis=0).astype(BF16)
             gl[rows, :] = jnp.concatenate([lo[:, :128], lo[:, 128:]], axis=0).astype(BF16)
 
+        each(U_IN, gather_cells)
+
         for i in range(4):
             rows = slice(i * 64, i * 64 + 64)
             wide = dot(gh[rows, :], rep[...]) + dot(gl[rows, :], rep[...])
             xin[rows, :] = (wide * fr8[rows, :]).astype(BF16)
 
-        @pl.loop(0, CHUNKS)
-        def _(m):
+        def forward(m):
             rows = pl.ds(mo(m * 16, 16), 16)
             for half in range(2):
                 span = slice(half * 256, half * 256 + DOF)
                 x = xin[rows, span]
-                o0 = dot(x, blk[4 * m + half], NT)
-                o1 = dot(x, blk[4 * m + 2 + half], NT)
+                o0 = dot(x, blk[2 * m + PAIRS * half], NT)
+                o1 = dot(x, blk[2 * m + 1 + PAIRS * half], NT)
                 fw[rows, span] = jnp.where(row16, o0, o1).astype(BF16)
+
+        each(U_PROD, forward)
 
         for i in range(4):
             rows = slice(i * 64, i * 64 + 64)
@@ -284,9 +341,9 @@
         acce[...] = jnp.zeros(acce.shape, F32)
         acci[...] = jnp.zeros(acci.shape, F32)
 
-        @pl.loop(0, CHUNKS)
-        def _(m):
-            acce[...] += scatter_nodes(m, EDGE)
+        @pl.loop(0, CHUNKS // U_EDGE)
+        def _(n):
+            acce[...] += scatter_nodes(n, U_EDGE, EDGE)
 
         swap = [
             rcopy(acce.at[pl.ds(0, 48), :], renext.at[h], e_s.at[h, 0], e_r.at[h, 0], (prv, group)),
@@ -295,9 +352,9 @@
         for cpy in swap:
             cpy.start()
 
-        @pl.loop(0, CHUNKS)
-        def _(m):
-            acci[...] += scatter_nodes(m, INNER)
+        @pl.loop(0, CHUNKS // U_INNER)
+        def _(n):
+            acci[...] += scatter_nodes(n, U_INNER, INNER)
 
         if h > 0:
             square_mid(h - 1)
@@ -306,11 +363,10 @@
             pair = []
             for j in range(2):
                 n = 2 * i + j
-                pair.append(acci[n * 8 : n * 8 + 8, :] * w_ref[6 + n : 7 + n, :])
+                pair.append(acci[n * 8 : n * 8 + 8, :] * weight(w3, 6 + n))
             ti[i * 16 : i * 16 + 16, :] = jnp.concatenate(pair, axis=0).astype(BF16)
 
-        @pl.loop(0, CHUNKS)
-        def _(m):
+        def gather_inner(m):
             zero = jnp.zeros((8, 256), F32)
             out = gather_nodes(m, ti, INNER, [zero] * 3)
             r0 = mo(m * 16, 16)
@@ -318,6 +374,8 @@
                 span = slice(c * 128, c * 128 + 128)
                 ad1[pl.ds(r0, 8), span] = out[c][:, :128]
                 ad1[pl.ds(r0 + 8, 8), span] = out[c][:, 128:]
+
+        each(U_GET, gather_inner)
 
         for cpy in swap:
             cpy.wait()
@@ -327,15 +385,14 @@
                 n = 2 * i + j
                 if n < 6:
                     total = acce[n * 8 : n * 8 + 8, :] + reprev[h, n * 8 : n * 8 + 8, :] * has_prev
-                    pair.append(total * w_ref[n : n + 1, :])
+                    pair.append(total * weight(w3, n))
                 else:
                     o = (n - 6) * 8
                     total = acce[n * 8 : n * 8 + 8, :] + renext[h, o : o + 8, :]
-                    pair.append(total * (wn[n - 6 : n - 5, :] * has_next))
+                    pair.append(total * (weight(wn, n - 6) * has_next))
             te[i * 16 : i * 16 + 16, :] = jnp.concatenate(pair, axis=0).astype(BF16)
 
-        @pl.loop(0, CHUNKS)
-        def _(m):
+        def gather_edge(m):
             r0 = mo(m * 16, 16)
             base = []
             for c in range(3):
@@ -350,36 +407,46 @@
                     [out[c][:, :128], out[c][:, 128:]], axis=0
                 ).astype(BF16)
 
+        each(U_GET, gather_edge)
+
         for i in range(4):
             rows = slice(i * 64, i * 64 + 64)
             ain[rows, :] = dot(ad[rows, :], pm[...]).astype(BF16)
 
-        @pl.loop(0, CHUNKS)
-        def _(m):
+        def adjoint(m):
             rows = pl.ds(mo(m * 16, 16), 16)
             for half in range(2):
                 span = slice(half * 256, half * 256 + DOF)
                 x = ain[rows, span]
-                o0 = dot(x, blk[4 * m + half])
-                o1 = dot(x, blk[4 * m + 2 + half])
+                o0 = dot(x, blk[2 * m + PAIRS * half])
+                o1 = dot(x, blk[2 * m + 1 + PAIRS * half])
                 hi, lo = split(jnp.where(row16, o0, o1) * fr8[rows, span])
                 yh[rows, span] = hi.astype(BF16)
                 yl[rows, span] = lo.astype(BF16)
 
+        each(U_PROD, adjoint)
+
         for i in range(4):
             rows = slice(i * 64, i * 64 + 64)
             pt[rows, :] = dot(yh[rows, :], sel[...]) + dot(yl[rows, :], sel[...])
 
-        def scatter_cells(m, acc):
-            r0 = mo(m * 16, 16)
-            v = jnp.concatenate([pt[pl.ds(r0, 8), :], pt[pl.ds(r0 + 8, 8), :]], axis=1)
-            a = ac8[pl.ds(mo(m * 8, 8), 8), :]
-            spread = jnp.concatenate(
-                [jnp.where(a == lv, s, 0.0) for lv in range(3) for s in split(v)], axis=0
+        def scatter_cells(n, acc):
+            spreads = []
+            for j in range(U_PUT):
+                m = n * U_PUT + j
+                r0 = mo(m * 16, 16)
+                v = jnp.concatenate([pt[pl.ds(r0, 8), :], pt[pl.ds(r0 + 8, 8), :]], axis=1)
+                a = ac8[pl.ds(mo(m * 8, 8), 8), :]
+                spread = jnp.concatenate(
+                    [jnp.where(a == lv, s, 0.0) for lv in range(3) for s in split(v)], axis=0
+                )
+                spreads.append(spread.astype(BF16))
+            size = U_PUT * 256
+            return acc + dot(
+                jnp.concatenate(spreads, axis=1), ohct[pl.ds(mo(n * size, size), size), :]
             )
-            return acc + dot(spread.astype(BF16), ohct[pl.ds(mo(m * 256, 256), 256), :])
-
-        acc = lax.fori_loop(0, CHUNKS, scatter_cells, jnp.zeros((48, 128), F32))
+
+        acc = lax.fori_loop(0, CHUNKS // U_PUT, scatter_cells, jnp.zeros((48, 128), F32))
         sums = [acc[n * 16 : n * 16 + 8] + acc[n * 16 + 8 : n * 16 + 16] for n in range(3)]
         bs[h, 0] = sums[0]
         bs[h, 1] = sums[2]
@@ -428,63 +495,53 @@
     member = one(lax.broadcasted_iota(I32, (64, 256), 0) == cl_ref[...])
     gk[...] = dot(member, hi.astype(BF16), NT) + dot(member, lo.astype(BF16), NT)
 
-    ka[my_z] = gk[pl.ds(mo(my_z * 8, 8), 8), :]
+    ka[my_yx] = gk[pl.ds(mo(my_yx * 8, 8), 8), :]
+    for d in range(1, YXS):
+        yx = yx_peer(d)
+        rcopy(
+            gk.at[pl.ds(mo(yx * 8, 8), 8), :], ka.at[my_yx], k_s.at[0, d], k_r.at[0, my_yx],
+            yx_device(yx),
+        ).start()
+    for d in range(1, YXS):
+        yx = yx_peer(d)
+        got = rcopy(ka.at[yx], ka.at[yx], k_s.at[0, d], k_r.at[0, yx], yx_device(yx))
+        got.wait_recv()
+        got.wait_send()
+    total = ka[0]
+    for yx in range(1, YXS):
+        total = total + ka[yx]
+    kb[my_z] = total
     for d in range(1, ZS):
-        z = z_peer(d)
         rcopy(
-            gk.at[pl.ds(mo(z * 8, 8), 8), :], ka.at[my_z], k_s.at[0, d], k_r.at[0, my_z],
-            z_device(z),
+            kb.at[my_z], kb.at[my_z], k_s.at[1, d], k_r.at[1, my_z], z_device(z_peer(d))
         ).start()
     for d in range(1, ZS):
         z = z_peer(d)
-        got = rcopy(ka.at[z], ka.at[z], k_s.at[0, d], k_r.at[0, z], z_device(z))
+        got = rcopy(kb.at[z], kb.at[z], k_s.at[1, d], k_r.at[1, z], z_device(z))
         got.wait_recv()
         got.wait_send()
-    total = ka[0]
+    total = kb[0]
     for z in range(1, ZS):
-        total = total + ka[z]
-    kb[my_yx] = total
+        total = total + kb[z]
+    kc[my_yx] = total
     for d in range(1, YXS):
         rcopy(
-            kb.at[my_yx], kb.at[my_yx], k_s.at[1, d], k_r.at[1, my_yx], yx_device(yx_peer(d))
+            kc.at[my_yx], kc.at[my_yx], k_s.at[2, d], k_r.at[2, my_yx], yx_device(yx_peer(d))
         ).start()
     for d in range(1, YXS):
         yx = yx_peer(d)
-        got = rcopy(kb.at[yx], kb.at[yx], k_s.at[1, d], k_r.at[1, yx], yx_device(yx))
+        got = rcopy(kc.at[yx], kc.at[yx], k_s.at[2, d], k_r.at[2, yx], yx_device(yx))
         got.wait_recv()
         got.wait_send()
-    total = kb[0]
-    for yx in range(1, YXS):
-        total = total + kb[yx]
-    kc[my_z] = total
-    for d in range(1, ZS):
-        rcopy(
-            kc.at[my_z], kc.at[my_z], k_s.at[2, d], k_r.at[2, my_z], z_device(z_peer(d))
-        ).start()
-    for d in range(1, ZS):
-        z = z_peer(d)
-        got = rcopy(kc.at[z], kc.at[z], k_s.at[2, d], k_r.at[2, z], z_device(z))
-        got.wait_recv()
-        got.wait_send()
-    for z in range(ZS):
-        gram_ref[z * 8 : z * 8 + 8, :] = kc[z]
+    for yx in range(YXS):
+        gram_ref[yx * 8 : yx * 8 + 8, :] = kc[yx]
 
 
 def shards(
     blocks, connectivity, basal_map, friction, elem_counts, obs_weight, sign_bits, cluster_ids
 ):
-    live = jnp.arange(ELEMS, dtype=I32) < elem_counts[0]
-    fr = jnp.where(live[:, None], friction.reshape(ELEMS, DOF), 0.0)
-    fr = jnp.pad(fr, ((0, 0), (0, 256 - DOF))).reshape(PAIRS, 512)
-    idx = jnp.concatenate([connectivity.reshape(PAIRS, 128), basal_map.reshape(PAIRS, 128)], axis=0)
-    w = obs_weight.reshape(16, 256, 3).transpose(0, 2, 1).reshape(48, 256)
-    parity = jnp.arange(8, dtype=I32)[:, None] % 2
-    same = (cluster_ids % 2)[None, :] == parity
-    start = jnp.where(same, (2 * sign_bits.T - 1).astype(F32), 0.0)
-    qs = jnp.pad(jnp.concatenate([start, same.astype(F32)], axis=0), ((0, 0), (RIM, RIM)))
-    cl = cluster_ids.reshape(1, 256)
-
     vmem = pl.BlockSpec(memory_space=pltpu.VMEM)
+    here = pl.BlockSpec(memory_space=pl.ANY)
     dma = pltpu.SemaphoreType.DMA
     samp, refd, gram = pl.pallas_call(
         kernel,
@@ -493,9 +550,17 @@
             jax.ShapeDtypeStruct((8, 384), F32),
             jax.ShapeDtypeStruct((64, 256), F32),
         ),
-        in_specs=[pl.BlockSpec(memory_space=pl.ANY)] + [vmem] * 5,
+        in_specs=[here] * 4 + [pl.BlockSpec(memory_space=pltpu.SMEM)] + [here] * 3,
         out_specs=(vmem, vmem, vmem),
         scratch_shapes=[
+            pltpu.VMEM((ELEMS, 64), I32),
+            pltpu.VMEM((ELEMS, 64), I32),
+            pltpu.VMEM((3, ELEMS, 64), F32),
+            pltpu.VMEM((3, 4096), F32),
+            pltpu.VMEM((8, 256), I32),
+            pltpu.VMEM((1, 256), I32),
+            pltpu.VMEM((ELEMS, 128), I32),
+            pltpu.VMEM((16, 384), F32),
             pltpu.VMEM((ELEMS, DOF, DOF), BF16),
             pltpu.VMEM((256, 4096), BF16),
             pltpu.VMEM((4096, 256), BF16),
@@ -523,7 +588,7 @@
             pltpu.VMEM((256, 512), BF16),
             pltpu.VMEM((256, 512), BF16),
             pltpu.VMEM((256, 128), F32),
-            pltpu.VMEM((8, 256), F32),
+            pltpu.VMEM((3, 512), F32),
             pltpu.VMEM((16, 128), F32),
             pltpu.VMEM((16, 128), F32),
             pltpu.VMEM((ROUNDS, 48, 256), F32),
@@ -539,6 +604,7 @@
             pltpu.VMEM((YXS, 8, 256), F32),
             pltpu.VMEM((ZS, 8, 256), F32),
             dma,
+            dma((6,)),
             dma((3,)),
             dma((3,)),
             dma((ROUNDS, 2)),
@@ -553,9 +619,12 @@
             dma((3, 8)),
         ],
         compiler_params=pltpu.CompilerParams(
-            collective_id=0, has_side_effects=True, vmem_limit_bytes=48 * 1024 * 1024
+            collective_id=0, has_side_effects=True, vmem_limit_bytes=63 * 1024 * 1024
         ),
-    )(blocks, idx, fr, w, qs, cl)
+    )(
+        blocks, connectivity, basal_map, friction.transpose(2, 0, 1), elem_counts,
+        obs_weight.T, sign_bits.T, cluster_ids[None, :],
+    )
     samples = samp[:, RIM : RIM + 256].T
     refined = refd[:, RIM : RIM + 256].T
     return samples, refined, gram.reshape(64, 8, 32)

time: 129 us -> 81.7 us (0.63)
  Pallas kernels: 119 us -> 77.1 us
  local copies, waits for them, and re-layouts: 5.78 us -> 2.99 us
  other arithmetic: 1.63 us -> 0 us
    pallas_call x1, Pallas kernels: 119 us -> 77.1 us  [shards(): pl.pallas_call(kernel, out_shape=(jax.ShapeDtypeStruct((8, 384), F32), ja...]
    reshape x5 -> x0, local copies, waits for them, and re-layouts: 2.59 us -> none  [the longest x1 0.86 us: shards(): w = obs_weight.reshape(16, 256, 3).transpose(0, 2, 1).reshape(48, 256)]
    unnamed x4 -> x0, local copies, waits for them, and re-layouts: 1.75 us -> none
    select_n x4 -> x0, other arithmetic: 1.47 us -> none  [the longest x1 0.77 us: shards(): start = jnp.where(same, (2 * sign_bits.T - 1).astype(F32), 0.0)]
where the time goes in v2:
time: 81.7 us; the launch traced here: 81.4 us
  Pallas kernels  77.1 us (94%)
  local copies, waits for them, and re-layouts  2.99 us (4%)
  between operations  1.29 us (2%)
    pallas_call x1, Pallas kernels, shards(): pl.pallas_call(kernel, out_shape=(jax.ShapeDtypeStruct((8, 384), F32), ja...  77.1 us

profile of v2, /device:TPU:2, one launch (start us, length us, event | category | flops | bytes accessed | tf_op | source)
XLA Modules:
  0.0 81.4 jit_solution(8991345310133530966)
XLA Ops:
  1.3 77.1 %shard_map.103 = (f32[8,384]{1,0:T(8,128)}, f32[8,384]{1,0:T(8,128)}, f32[64,256]{1,0:T(8,128)}) custom-call(bf16[64,192,192]{2,1,0:T(8,128)(2,1)} %blk_hbm.1, s32[64,64]{1,0:T(8,128)} %conn_hbm.1, s32[64,64]{1,0:T(8,128)} %cell_hbm.1, f32[3,64,64]{2,1,0:T(8,128)} %bitcast.10, s32[1]{0:T(128)S(6)} %copy.13.count_ref, f32[3,4096]{1,0:T(4,128)} %bitcast.11, ...), custom_call_target="tpu_custom_call" | custom-call | tf_op jit(solution)/shard_map/pallas_call | solution.py:546
  78.4 1.4 %slice_bitcast_fusion = (f32[256,8]{0,1:T(8,128)}, f32[256,8]{0,1:T(8,128)}) fusion(f32[8,384]{1,0:T(8,128)} %get-tuple-element.7, f32[8,384]{1,0:T(8,128)} %get-tuple-element.6), kind=kLoop, calls=%fused_computation | loop fusion | bytes 32768 | tf_op jit(solution)/shard_map/transpose | solution.py:629
  79.8 1.6 %copy.12 = f32[64,256]{0,1:T(8,128)} copy(f32[64,256]{1,0:T(8,128)} %get-tuple-element.8) | data formatting | bytes 131072 | tf_op jit(solution)/shard_map/pallas_call | solution.py:546

commit v3 on v2

--- a/solution.py
+++ b/solution.py
@@ -21,7 +21,7 @@
 U_PROD = 16
 U_EDGE = 16
 U_INNER = 16
-U_GET = 16
+U_GET = 8
 U_PUT = 16
 ZS = 8
 YXS = 8
@@ -37,8 +37,8 @@
     return pl.multiple_of(x, n)
 
 
-def each(unroll, body):
-    @pl.loop(0, CHUNKS // unroll)
+def each(unroll, body, steps=CHUNKS):
+    @pl.loop(0, steps // unroll)
     def _(n):
         for j in range(unroll):
             body(n * unroll + j)
@@ -57,9 +57,9 @@
     blk_hbm, conn_hbm, cell_hbm, fr_hbm, count_ref, w_hbm, sign_hbm, cl_hbm,
     samp_ref, refd_ref, gram_ref,
     conn, cell, fr3, w3, sign, cl_ref, idx_ref, qs_ref,
-    blk, ohn, ohnt, ohc, ohct, an8, ac8, fr8, rep, sel, pm, pmt,
+    blk, ohn, ohc, an8, ac8, fr8, rep, sel, pm, pmt,
     gh, gl, xin, fw, fc, acce, acci, te, ti, ad1, ad, ain, yh, yl, pt,
-    wn, qsp, qsn, renext, reprev, bs, rbn, rbp, pa, pb, cp, gk, ka, kb, kc,
+    wn, qsp, qsn, esend, renext, reprev, bs, rbn, rbp, pa, pb, fp, fpn, fpp, gk, ka, kb, kc,
     blk_sem, in_sem, i_s, i_r, e_s, e_r, b_s, b_r, p_s, p_r, g_s, g_r, k_s, k_r,
 ):
     tile = lax.axis_index("tiles")
@@ -112,7 +112,10 @@
     for d in range(1, YXS):
         greet(yx_device(yx_peer(d)))
     for d in range(1, GROUPS):
-        greet((tile, lax.rem(group + d, GROUPS)))
+        other = lax.rem(group + d, GROUPS)
+        greet((tile, other))
+        greet((nxt, other))
+        greet((prv, other))
 
     def one(cond):
         return jnp.where(cond, 1.0, 0.0).astype(BF16)
@@ -154,7 +157,7 @@
         rcopy(qs_ref.at[:, pl.ds(0, 128)], qsn, i_s.at[1], i_r.at[1], (prv, group)),
         rcopy(w3.at[:, pl.ds(0, 512)], wn, i_s.at[2], i_r.at[2], (prv, group)),
     ]
-    pl.semaphore_wait(barrier, 2 + ZS - 1 + YXS - 1 + GROUPS - 1)
+    pl.semaphore_wait(barrier, 2 + ZS - 1 + YXS - 1 + 3 * (GROUPS - 1))
     for cpy in first:
         cpy.start()
 
@@ -184,20 +187,12 @@
             an8[rows, lanes] = jnp.broadcast_to(idx_ref[n : n + 1, :] >> 8, (8, 128))
             ac8[rows, lanes] = jnp.broadcast_to(idx_ref[PAIRS + n : PAIRS + n + 1, :] >> 7, (8, 128))
 
-    low = jnp.where(
-        lax.broadcasted_iota(I32, (64, 128), 0) < PAIRS, idx_ref[...] & 255, idx_ref[...] & 127
-    ).astype(F32)
-    cols = jnp.transpose(jnp.concatenate([low, jnp.zeros((64, 128), F32)], axis=0))
     sub_n = lax.broadcasted_iota(I32, (256, 128), 0)
     sub_c = lax.broadcasted_iota(I32, (128, 128), 0)
-    lane_n = lax.broadcasted_iota(I32, (128, 256), 1).astype(F32)
-    lane_c = lax.broadcasted_iota(I32, (128, 128), 1).astype(F32)
     for i in range(PAIRS):
         span = slice(i * 128, i * 128 + 128)
         ohn[:, span] = one(sub_n == (idx_ref[i : i + 1, :] & 255))
         ohc[:, span] = one(sub_c == (idx_ref[PAIRS + i : PAIRS + i + 1, :] & 127))
-        ohnt[span, :] = one(lane_n == cols[:, i : i + 1])
-        ohct[span, :] = one(lane_c == cols[:, PAIRS + i : PAIRS + i + 1])
 
     for cpy in first:
         cpy.wait()
@@ -284,11 +279,12 @@
             )
             spreads.append(spread.astype(BF16))
         size = unroll * 256
-        return dot(jnp.concatenate(spreads, axis=1), ohnt[pl.ds(mo(n * size, size), size), :])
+        return dot(jnp.concatenate(spreads, axis=1), ohn[:, pl.ds(mo(n * size, size), size)], NT)
 
     def gather_nodes(m, table, levels, base):
-        got = dot(table[...], ohn[:, pl.ds(mo(m * 256, 256), 256)])
-        a = an8[pl.ds(mo(m * 8, 8), 8), :]
+        got = dot(table[...], ohn[:, pl.ds(mo(m * 512, 512), 512)])
+        r = mo(m * 16, 16)
+        a = jnp.concatenate([an8[pl.ds(r, 8), :], an8[pl.ds(r + 8, 8), :]], axis=1)
         out = list(base)
         for n, lv in enumerate(levels):
             hit = a == lv
@@ -345,9 +341,10 @@
         def _(n):
             acce[...] += scatter_nodes(n, U_EDGE, EDGE)
 
+        esend[h] = acce[...].astype(BF16)
         swap = [
-            rcopy(acce.at[pl.ds(0, 48), :], renext.at[h], e_s.at[h, 0], e_r.at[h, 0], (prv, group)),
-            rcopy(acce.at[pl.ds(48, 48), :], reprev.at[h], e_s.at[h, 1], e_r.at[h, 1], (nxt, group)),
+            rcopy(esend.at[h, pl.ds(0, 48), :], renext.at[h], e_s.at[h, 0], e_r.at[h, 0], (prv, group)),
+            rcopy(esend.at[h, pl.ds(48, 48), :], reprev.at[h], e_s.at[h, 1], e_r.at[h, 1], (nxt, group)),
         ]
         for cpy in swap:
             cpy.start()
@@ -367,47 +364,47 @@
             ti[i * 16 : i * 16 + 16, :] = jnp.concatenate(pair, axis=0).astype(BF16)
 
         def gather_inner(m):
-            zero = jnp.zeros((8, 256), F32)
+            zero = jnp.zeros((8, 512), F32)
             out = gather_nodes(m, ti, INNER, [zero] * 3)
-            r0 = mo(m * 16, 16)
+            r0 = mo(m * 32, 32)
             for c in range(3):
                 span = slice(c * 128, c * 128 + 128)
-                ad1[pl.ds(r0, 8), span] = out[c][:, :128]
-                ad1[pl.ds(r0 + 8, 8), span] = out[c][:, 128:]
-
-        each(U_GET, gather_inner)
+                for j in range(4):
+                    ad1[pl.ds(r0 + 8 * j, 8), span] = out[c][:, j * 128 : j * 128 + 128]
+
+        each(U_GET, gather_inner, CHUNKS // 2)
 
         for cpy in swap:
             cpy.wait()
         for i in range(6):
+            if i < 3:
+                theirs = reprev[h, i * 16 : i * 16 + 16, :].astype(F32) * has_prev
+            else:
+                theirs = renext[h, i * 16 - 48 : i * 16 - 32, :].astype(F32)
+            total = acce[i * 16 : i * 16 + 16, :] + theirs
             pair = []
             for j in range(2):
                 n = 2 * i + j
-                if n < 6:
-                    total = acce[n * 8 : n * 8 + 8, :] + reprev[h, n * 8 : n * 8 + 8, :] * has_prev
-                    pair.append(total * weight(w3, n))
-                else:
-                    o = (n - 6) * 8
-                    total = acce[n * 8 : n * 8 + 8, :] + renext[h, o : o + 8, :]
-                    pair.append(total * (weight(wn, n - 6) * has_next))
+                scale = weight(w3, n) if n < 6 else weight(wn, n - 6) * has_next
+                pair.append(total[j * 8 : j * 8 + 8] * scale)
             te[i * 16 : i * 16 + 16, :] = jnp.concatenate(pair, axis=0).astype(BF16)
 
         def gather_edge(m):
-            r0 = mo(m * 16, 16)
+            r0 = mo(m * 32, 32)
             base = []
             for c in range(3):
                 span = slice(c * 128, c * 128 + 128)
                 base.append(
-                    jnp.concatenate([ad1[pl.ds(r0, 8), span], ad1[pl.ds(r0 + 8, 8), span]], axis=1)
+                    jnp.concatenate([ad1[pl.ds(r0 + 8 * j, 8), span] for j in range(4)], axis=1)
                 )
             out = gather_nodes(m, te, EDGE, base)
             for c in range(3):
                 span = slice(c * 128, c * 128 + 128)
-                ad[pl.ds(r0, 16), span] = jnp.concatenate(
-                    [out[c][:, :128], out[c][:, 128:]], axis=0
+                ad[pl.ds(r0, 32), span] = jnp.concatenate(
+                    [out[c][:, j * 128 : j * 128 + 128] for j in range(4)], axis=0
                 ).astype(BF16)
 
-        each(U_GET, gather_edge)
+        each(U_GET, gather_edge, CHUNKS // 2)
 
         for i in range(4):
             rows = slice(i * 64, i * 64 + 64)
@@ -443,11 +440,17 @@
                 spreads.append(spread.astype(BF16))
             size = U_PUT * 256
             return acc + dot(
-                jnp.concatenate(spreads, axis=1), ohct[pl.ds(mo(n * size, size), size), :]
+                jnp.concatenate(spreads, axis=1), ohc[:, pl.ds(mo(n * size, size), size)], NT
             )
 
         acc = lax.fori_loop(0, CHUNKS // U_PUT, scatter_cells, jnp.zeros((48, 128), F32))
         sums = [acc[n * 16 : n * 16 + 8] + acc[n * 16 + 8 : n * 16 + 16] for n in range(3)]
+        keep = same if h % 2 == 1 else [exist[n] - same[n] for n in range(3)]
+        if h == POWER:
+            scale = square_end(h - 1)
+            for n in range(3):
+                fp[group, :, n * 128 : n * 128 + 128] = sums[n] * keep[n] * scale
+            return None
         bs[h, 0] = sums[0]
         bs[h, 1] = sums[2]
         swap = [
@@ -461,7 +464,6 @@
             cpy.wait()
         sums[0] = sums[0] + rbp[h] * has_prev
         sums[2] = sums[2] + rbn[h] * has_next
-        keep = same if h % 2 == 1 else [exist[n] - same[n] for n in range(3)]
         out = []
         for n in range(3):
             v = sums[n] * keep[n]
@@ -475,31 +477,51 @@
         if h == 0:
             for n in range(3):
                 samp_ref[:, n * 128 : n * 128 + 128] = q[n]
-    for n in range(3):
-        refd_ref[:, n * 128 : n * 128 + 128] = q[n]
-
+    def final(kind, d, source):
+        other = lax.rem(group + d, GROUPS)
+        device, landing, span = (
+            ((prv, other), fpn, pl.ds(0, 128)),
+            ((nxt, other), fpp, pl.ds(256, 128)),
+            ((tile, other), fp, pl.ds(0, 384)),
+        )[kind]
+        return rcopy(
+            fp.at[group, :, span], landing.at[source], g_s.at[kind, d], g_r.at[kind, source], device
+        )
+
+    order = [(kind, d) for d in range(GROUPS) for kind in range(3) if kind < 2 or d > 0]
+    for kind, d in order:
+        final(kind, d, group).start()
+    for kind, d in order:
+        final(kind, d, lax.rem(group + d, GROUPS)).wait_recv()
+    for kind, d in order:
+        final(kind, d, group).wait_send()
+
+    def window(g):
+        return jnp.concatenate(
+            [
+                fp[g, :, 0:128] + fpp[g] * has_prev,
+                fp[g, :, 128:256],
+                fp[g, :, 256:384] + fpn[g] * has_next,
+            ],
+            axis=1,
+        )
+
+    refd_ref[...] = window(group)
     mine = pltpu.roll(refd_ref[...], 384 - RIM, 1)[:, :256]
-    cp[group] = mine
-    for d in range(1, GROUPS):
-        rcopy(
-            cp.at[group], cp.at[group], g_s.at[d], g_r.at[group], (tile, lax.rem(group + d, GROUPS))
-        ).start()
-    for d in range(1, GROUPS):
-        g = lax.rem(group + d, GROUPS)
-        got = rcopy(cp.at[g], cp.at[g], g_s.at[d], g_r.at[g], (tile, g))
-        got.wait_recv()
-        got.wait_send()
-    every = jnp.concatenate([cp[g] for g in range(GROUPS)], axis=0)
+    every = jnp.concatenate([window(g) for g in range(GROUPS)], axis=0)
+    every = pltpu.roll(every, 384 - RIM, 1)[:, :256]
     outer = jnp.concatenate([every * mine[i : i + 1, :] for i in range(8)], axis=0)
     hi, lo = split(outer)
     member = one(lax.broadcasted_iota(I32, (64, 256), 0) == cl_ref[...])
-    gk[...] = dot(member, hi.astype(BF16), NT) + dot(member, lo.astype(BF16), NT)
-
-    ka[my_yx] = gk[pl.ds(mo(my_yx * 8, 8), 8), :]
+    grams = dot(member, hi.astype(BF16), NT) + dot(member, lo.astype(BF16), NT)
+    for yx in range(YXS):
+        rows = grams[yx * 8 : yx * 8 + 8]
+        gk[yx] = jnp.concatenate([rows[:, :128], rows[:, 128:]], axis=0).astype(BF16)
+
     for d in range(1, YXS):
         yx = yx_peer(d)
         rcopy(
-            gk.at[pl.ds(mo(yx * 8, 8), 8), :], ka.at[my_yx], k_s.at[0, d], k_r.at[0, my_yx],
+            gk.at[yx], ka.at[my_yx], k_s.at[0, d], k_r.at[0, my_yx],
             yx_device(yx),
         ).start()
     for d in range(1, YXS):
@@ -507,10 +529,11 @@
         got = rcopy(ka.at[yx], ka.at[yx], k_s.at[0, d], k_r.at[0, yx], yx_device(yx))
         got.wait_recv()
         got.wait_send()
-    total = ka[0]
+    ka[my_yx] = gk[my_yx]
+    total = ka[0].astype(F32)
     for yx in range(1, YXS):
-        total = total + ka[yx]
-    kb[my_z] = total
+        total = total + ka[yx].astype(F32)
+    kb[my_z] = total.astype(BF16)
     for d in range(1, ZS):
         rcopy(
             kb.at[my_z], kb.at[my_z], k_s.at[1, d], k_r.at[1, my_z], z_device(z_peer(d))
@@ -520,9 +543,9 @@
         got = rcopy(kb.at[z], kb.at[z], k_s.at[1, d], k_r.at[1, z], z_device(z))
         got.wait_recv()
         got.wait_send()
-    total = kb[0]
+    total = kb[0].astype(F32)
     for z in range(1, ZS):
-        total = total + kb[z]
+        total = total + kb[z].astype(F32)
     kc[my_yx] = total
     for d in range(1, YXS):
         rcopy(
@@ -534,14 +557,15 @@
         got.wait_recv()
         got.wait_send()
     for yx in range(YXS):
-        gram_ref[yx * 8 : yx * 8 + 8, :] = kc[yx]
+        gram_ref[yx * 8 : yx * 8 + 8, 0:128] = kc[yx, 0:8]
+        gram_ref[yx * 8 : yx * 8 + 8, 128:256] = kc[yx, 8:16]
 
 
 def shards(
     blocks, connectivity, basal_map, friction, elem_counts, obs_weight, sign_bits, cluster_ids
 ):
     vmem = pl.BlockSpec(memory_space=pltpu.VMEM)
-    here = pl.BlockSpec(memory_space=pl.ANY)
+    here = pl.BlockSpec(memory_space=pltpu.HBM)
     dma = pltpu.SemaphoreType.DMA
     samp, refd, gram = pl.pallas_call(
         kernel,
@@ -563,9 +587,7 @@
             pltpu.VMEM((16, 384), F32),
             pltpu.VMEM((ELEMS, DOF, DOF), BF16),
             pltpu.VMEM((256, 4096), BF16),
-            pltpu.VMEM((4096, 256), BF16),
             pltpu.VMEM((128, 4096), BF16),
-            pltpu.VMEM((4096, 128), BF16),
             pltpu.VMEM((128, 256), I32),
             pltpu.VMEM((128, 256), I32),
             pltpu.VMEM((256, 512), F32),
@@ -591,18 +613,21 @@
             pltpu.VMEM((3, 512), F32),
             pltpu.VMEM((16, 128), F32),
             pltpu.VMEM((16, 128), F32),
-            pltpu.VMEM((ROUNDS, 48, 256), F32),
-            pltpu.VMEM((ROUNDS, 48, 256), F32),
+            pltpu.VMEM((ROUNDS, 96, 256), BF16),
+            pltpu.VMEM((ROUNDS, 48, 256), BF16),
+            pltpu.VMEM((ROUNDS, 48, 256), BF16),
             pltpu.VMEM((ROUNDS, 2, 8, 128), F32),
             pltpu.VMEM((ROUNDS, 8, 128), F32),
             pltpu.VMEM((ROUNDS, 8, 128), F32),
             pltpu.VMEM((POWER, ZS, 8, 128), F32),
             pltpu.VMEM((POWER, YXS, 8, 128), F32),
-            pltpu.VMEM((GROUPS, 8, 256), F32),
-            pltpu.VMEM((64, 256), F32),
-            pltpu.VMEM((ZS, 8, 256), F32),
-            pltpu.VMEM((YXS, 8, 256), F32),
-            pltpu.VMEM((ZS, 8, 256), F32),
+            pltpu.VMEM((GROUPS, 8, 384), F32),
+            pltpu.VMEM((GROUPS, 8, 128), F32),
+            pltpu.VMEM((GROUPS, 8, 128), F32),
+            pltpu.VMEM((YXS, 16, 128), BF16),
+            pltpu.VMEM((YXS, 16, 128), BF16),
+            pltpu.VMEM((ZS, 16, 128), BF16),
+            pltpu.VMEM((YXS, 16, 128), F32),
             dma,
             dma((6,)),
             dma((3,)),
@@ -613,13 +638,13 @@
             dma((ROUNDS, 2)),
             dma((POWER, 2, 8)),
             dma((POWER, 2, 8)),
-            dma((GROUPS,)),
-            dma((GROUPS,)),
+            dma((3, GROUPS)),
+            dma((3, GROUPS)),
             dma((3, 8)),
             dma((3, 8)),
         ],
         compiler_params=pltpu.CompilerParams(
-            collective_id=0, has_side_effects=True, vmem_limit_bytes=63 * 1024 * 1024
+            collective_id=0, has_side_effects=True, vmem_limit_bytes=48 * 1024 * 1024
         ),
     )(
         blocks, connectivity, basal_map, friction.transpose(2, 0, 1), elem_counts,

time: 81.7 us -> 82.5 us (level)
  local copies, waits for them, and re-layouts: 2.99 us -> 6.04 us
  Pallas kernels: 77.1 us -> 74.8 us
    unnamed x0 -> x12, local copies, waits for them, and re-layouts: none -> 4.61 us
    pallas_call x1, Pallas kernels: 77.1 us -> 74.8 us  [shards(): pl.pallas_call(kernel, out_shape=(jax.ShapeDtypeStruct((8, 384), F32), ja...]
    pallas_call x1, local copies, waits for them, and re-layouts: 1.59 us -> 0.75 us  [shards(): pl.pallas_call(kernel, out_shape=(jax.ShapeDtypeStruct((8, 384), F32), ja...]
where the time goes in v3:
time: 82.5 us; the launch traced here: 82.2 us
  Pallas kernels  74.8 us (91%)
  local copies, waits for them, and re-layouts  6.04 us (7%)
  between operations  1.3 us (2%)
    pallas_call x1, Pallas kernels, shards(): pl.pallas_call(kernel, out_shape=(jax.ShapeDtypeStruct((8, 384), F32), ja...  74.8 us
    unnamed x12, local copies, waits for them, and re-layouts  4.61 us

profile of v3, /device:TPU:2, one launch (start us, length us, event | category | flops | bytes accessed | tf_op | source)
XLA Modules:
  0.0 82.2 jit_solution(16668528238355991289)
XLA Ops:
  1.3 0.0 copy-start
  1.3 0.9 %copy-done = f32[64,64,3]{1,0,2:T(8,128)S(1)} copy-done((f32[64,64,3]{1,0,2:T(8,128)S(1)}, f32[64,64,3]{1,0,2:T(8,128)}, u32[]{:S(2)}) %copy-start) | copy-done | bytes 49176
  2.2 0.0 copy-start.1
  2.2 0.8 %copy-done.1 = f32[4096,3]{0,1:T(4,128)S(1)} copy-done((f32[4096,3]{0,1:T(4,128)S(1)}, f32[4096,3]{0,1:T(4,128)}, u32[]{:S(2)}) %copy-start.1) | copy-done | bytes 49176
  3.0 0.0 copy-start.2
  3.0 0.8 copy-done.2
  3.8 0.0 copy-start.3
  3.8 0.8 copy-done.3
  4.5 0.0 copy-start.4
  4.5 0.7 copy-done.4
  5.2 0.0 copy-start.5
  5.2 0.7 copy-done.5
  5.9 74.8 %shard_map.103 = (f32[8,384]{1,0:T(8,128)S(1)}, f32[8,384]{1,0:T(8,128)S(1)}, f32[64,256]{1,0:T(8,128)S(1)}) custom-call(bf16[64,192,192]{2,1,0:T(8,128)(2,1)} %blk_hbm.1, s32[64,64]{1,0:T(8,128)S(1)} %copy-done.2, s32[64,64]{1,0:T(8,128)S(1)} %copy-done.3, f32[3,64,64]{2,1,0:T(8,128)S(1)} %bitcast.9, s32[1]{0:T(128)S(6)} %copy.13.count_ref, ...), custom_call_target="tpu_custom_call" | custom-call | tf_op jit(solution)/shard_map/pallas_call | solution.py:570
  80.7 0.7 slice_bitcast_fusion
  81.4 0.8 copy.12
Async XLA Ops:
  1.3 0.9 %copy-start = (f32[64,64,3]{1,0,2:T(8,128)S(1)}, f32[64,64,3]{1,0,2:T(8,128)}, u32[]{:S(2)}) copy-start(f32[64,64,3]{1,0,2:T(8,128)} %param.11) | copy-start | bytes 147460
  2.2 0.8 %copy-start.1 = (f32[4096,3]{0,1:T(4,128)S(1)}, f32[4096,3]{0,1:T(4,128)}, u32[]{:S(2)}) copy-start(f32[4096,3]{0,1:T(4,128)} %param.13) | copy-start | bytes 147460
  3.0 0.8 copy-start.2
  3.8 0.8 copy-start.3
  4.5 0.7 copy-start.4
  5.2 0.7 copy-start.5

commit v4 on v3

--- a/solution.py
+++ b/solution.py
@@ -55,9 +55,9 @@
 
 def kernel(
     blk_hbm, conn_hbm, cell_hbm, fr_hbm, count_ref, w_hbm, sign_hbm, cl_hbm,
-    samp_ref, refd_ref, gram_ref,
+    out_ref, gram_ref,
     conn, cell, fr3, w3, sign, cl_ref, idx_ref, qs_ref,
-    blk, ohn, ohc, an8, ac8, fr8, rep, sel, pm, pmt,
+    blk, ohn, ohnt, ohc, ohct, an8, ac8, fr8, rep, sel, pm, pmt,
     gh, gl, xin, fw, fc, acce, acci, te, ti, ad1, ad, ain, yh, yl, pt,
     wn, qsp, qsn, esend, renext, reprev, bs, rbn, rbp, pa, pb, fp, fpn, fpp, gk, ka, kb, kc,
     blk_sem, in_sem, i_s, i_r, e_s, e_r, b_s, b_r, p_s, p_r, g_s, g_r, k_s, k_r,
@@ -187,12 +187,20 @@
             an8[rows, lanes] = jnp.broadcast_to(idx_ref[n : n + 1, :] >> 8, (8, 128))
             ac8[rows, lanes] = jnp.broadcast_to(idx_ref[PAIRS + n : PAIRS + n + 1, :] >> 7, (8, 128))
 
+    low = jnp.where(
+        lax.broadcasted_iota(I32, (64, 128), 0) < PAIRS, idx_ref[...] & 255, idx_ref[...] & 127
+    ).astype(F32)
+    cols = jnp.transpose(jnp.concatenate([low, jnp.zeros((64, 128), F32)], axis=0))
+    lane_n = lax.broadcasted_iota(I32, (128, 256), 1).astype(F32)
+    lane_c = lax.broadcasted_iota(I32, (128, 128), 1).astype(F32)
     sub_n = lax.broadcasted_iota(I32, (256, 128), 0)
     sub_c = lax.broadcasted_iota(I32, (128, 128), 0)
     for i in range(PAIRS):
         span = slice(i * 128, i * 128 + 128)
         ohn[:, span] = one(sub_n == (idx_ref[i : i + 1, :] & 255))
         ohc[:, span] = one(sub_c == (idx_ref[PAIRS + i : PAIRS + i + 1, :] & 127))
+        ohnt[span, :] = one(lane_n == cols[:, i : i + 1])
+        ohct[span, :] = one(lane_c == cols[:, PAIRS + i : PAIRS + i + 1])
 
     for cpy in first:
         cpy.wait()
@@ -279,7 +287,7 @@
             )
             spreads.append(spread.astype(BF16))
         size = unroll * 256
-        return dot(jnp.concatenate(spreads, axis=1), ohn[:, pl.ds(mo(n * size, size), size)], NT)
+        return dot(jnp.concatenate(spreads, axis=1), ohnt[pl.ds(mo(n * size, size), size), :])
 
     def gather_nodes(m, table, levels, base):
         got = dot(table[...], ohn[:, pl.ds(mo(m * 512, 512), 512)])
@@ -440,7 +448,7 @@
                 spreads.append(spread.astype(BF16))
             size = U_PUT * 256
             return acc + dot(
-                jnp.concatenate(spreads, axis=1), ohc[:, pl.ds(mo(n * size, size), size)], NT
+                jnp.concatenate(spreads, axis=1), ohct[pl.ds(mo(n * size, size), size), :]
             )
 
         acc = lax.fori_loop(0, CHUNKS // U_PUT, scatter_cells, jnp.zeros((48, 128), F32))
@@ -475,8 +483,7 @@
         if h < POWER:
             square_start(h, q)
         if h == 0:
-            for n in range(3):
-                samp_ref[:, n * 128 : n * 128 + 128] = q[n]
+            out_ref[0:8, :] = pltpu.roll(jnp.concatenate(q, axis=1), 384 - RIM, 1)[:, :256]
     def final(kind, d, source):
         other = lax.rem(group + d, GROUPS)
         device, landing, span = (
@@ -506,8 +513,8 @@
             axis=1,
         )
 
-    refd_ref[...] = window(group)
-    mine = pltpu.roll(refd_ref[...], 384 - RIM, 1)[:, :256]
+    mine = pltpu.roll(window(group), 384 - RIM, 1)[:, :256]
+    out_ref[8:16, :] = mine
     every = jnp.concatenate([window(g) for g in range(GROUPS)], axis=0)
     every = pltpu.roll(every, 384 - RIM, 1)[:, :256]
     outer = jnp.concatenate([every * mine[i : i + 1, :] for i in range(8)], axis=0)
@@ -565,17 +572,16 @@
     blocks, connectivity, basal_map, friction, elem_counts, obs_weight, sign_bits, cluster_ids
 ):
     vmem = pl.BlockSpec(memory_space=pltpu.VMEM)
-    here = pl.BlockSpec(memory_space=pltpu.HBM)
+    here = pl.BlockSpec(memory_space=pl.ANY)
     dma = pltpu.SemaphoreType.DMA
-    samp, refd, gram = pl.pallas_call(
+    cells, gram = pl.pallas_call(
         kernel,
         out_shape=(
-            jax.ShapeDtypeStruct((8, 384), F32),
-            jax.ShapeDtypeStruct((8, 384), F32),
+            jax.ShapeDtypeStruct((16, 256), F32),
             jax.ShapeDtypeStruct((64, 256), F32),
         ),
         in_specs=[here] * 4 + [pl.BlockSpec(memory_space=pltpu.SMEM)] + [here] * 3,
-        out_specs=(vmem, vmem, vmem),
+        out_specs=(vmem, vmem),
         scratch_shapes=[
             pltpu.VMEM((ELEMS, 64), I32),
             pltpu.VMEM((ELEMS, 64), I32),
@@ -587,7 +593,9 @@
             pltpu.VMEM((16, 384), F32),
             pltpu.VMEM((ELEMS, DOF, DOF), BF16),
             pltpu.VMEM((256, 4096), BF16),
+            pltpu.VMEM((4096, 256), BF16),
             pltpu.VMEM((128, 4096), BF16),
+            pltpu.VMEM((4096, 128), BF16),
             pltpu.VMEM((128, 256), I32),
             pltpu.VMEM((128, 256), I32),
             pltpu.VMEM((256, 512), F32),
@@ -644,15 +652,13 @@
             dma((3, 8)),
         ],
         compiler_params=pltpu.CompilerParams(
-            collective_id=0, has_side_effects=True, vmem_limit_bytes=48 * 1024 * 1024
+            collective_id=0, has_side_effects=True, vmem_limit_bytes=63 * 1024 * 1024
         ),
     )(
         blocks, connectivity, basal_map, friction.transpose(2, 0, 1), elem_counts,
         obs_weight.T, sign_bits.T, cluster_ids[None, :],
     )
-    samples = samp[:, RIM : RIM + 256].T
-    refined = refd[:, RIM : RIM + 256].T
-    return samples, refined, gram.reshape(64, 8, 32)
+    return cells[:8].T, cells[8:].T, gram.reshape(64, 8, 32)
 
 
 def solution(mesh):

time: 82.5 us -> 78.8 us (0.955)
  local copies, waits for them, and re-layouts: 6.04 us -> 2.91 us
    unnamed x12 -> x0, local copies, waits for them, and re-layouts: 4.61 us -> none
    pallas_call x1, local copies, waits for them, and re-layouts: 0.75 us -> 1.59 us  [shards(): pl.pallas_call(kernel, out_shape=(jax.ShapeDtypeStruct((16, 256), F32), j...]
where the time goes in v4:
time: 78.8 us; the launch traced here: 78.5 us
  Pallas kernels  74.3 us (94%)
  local copies, waits for them, and re-layouts  2.91 us (4%)
  between operations  1.29 us (2%)
    pallas_call x1, Pallas kernels, shards(): pl.pallas_call(kernel, out_shape=(jax.ShapeDtypeStruct((16, 256), F32), j...  74.3 us
    pallas_call x1, local copies, waits for them, and re-layouts, shards(): pl.pallas_call(kernel, out_shape=(jax.ShapeDtypeStruct((16, 256), F32), j...  1.59 us

profile of v4, /device:TPU:2, one launch (start us, length us, event | category | flops | bytes accessed | tf_op | source)
XLA Modules:
  0.0 78.5 jit_solution(14565141273155133523)
XLA Ops:
  1.3 74.3 %shard_map.103 = (f32[16,256]{1,0:T(8,128)}, f32[64,256]{1,0:T(8,128)}) custom-call(bf16[64,192,192]{2,1,0:T(8,128)(2,1)} %blk_hbm.1, s32[64,64]{1,0:T(8,128)} %conn_hbm.1, s32[64,64]{1,0:T(8,128)} %cell_hbm.1, f32[3,64,64]{2,1,0:T(8,128)} %bitcast.10, s32[1]{0:T(128)S(6)} %copy.13.count_ref, f32[3,4096]{1,0:T(4,128)} %bitcast.11, s32[8,256]{1,0:T(8,128)} %bitcast.12, ...), custom_call_target="tpu_custom_call" | custom-call | tf_op jit(solution)/shard_map/pallas_call | solution.py:577
  75.6 1.3 %slice_bitcast_fusion = (f32[256,8]{0,1:T(8,128)}, f32[256,8]{0,1:T(8,128)}) fusion(f32[16,256]{1,0:T(8,128)} %get-tuple-element.5), kind=kLoop, calls=%fused_computation | loop fusion | bytes 32768 | tf_op jit(solution)/shard_map/transpose | solution.py:661
  76.9 1.6 %copy.12 = f32[64,256]{0,1:T(8,128)} copy(f32[64,256]{1,0:T(8,128)} %get-tuple-element.6) | data formatting | bytes 131072 | tf_op jit(solution)/shard_map/pallas_call | solution.py:577

commit v5 on v4

--- a/solution.py
+++ b/solution.py
@@ -19,9 +19,9 @@
 CHUNKS = 16
 U_IN = 16
 U_PROD = 16
-U_EDGE = 16
-U_INNER = 16
-U_GET = 8
+U_EDGE = 8
+U_INNER = 8
+U_GET = 4
 U_PUT = 16
 ZS = 8
 YXS = 8
@@ -60,7 +60,7 @@
     blk, ohn, ohnt, ohc, ohct, an8, ac8, fr8, rep, sel, pm, pmt,
     gh, gl, xin, fw, fc, acce, acci, te, ti, ad1, ad, ain, yh, yl, pt,
     wn, qsp, qsn, esend, renext, reprev, bs, rbn, rbp, pa, pb, fp, fpn, fpp, gk, ka, kb, kc,
-    blk_sem, in_sem, i_s, i_r, e_s, e_r, b_s, b_r, p_s, p_r, g_s, g_r, k_s, k_r,
+    blk_sem, in_sem, i_s, i_r, e_s, e_r, b_s, b_r, s_s, p_r, g_s, g_r, k_r,
 ):
     tile = lax.axis_index("tiles")
     group = lax.axis_index("probes")
@@ -230,14 +230,14 @@
         pa[i, my_z] = total
         for d in range(1, ZS):
             rcopy(
-                pa.at[i, my_z], pa.at[i, my_z], p_s.at[i, 0, d], p_r.at[i, 0, my_z],
+                pa.at[i, my_z], pa.at[i, my_z], s_s.at[d], p_r.at[i, 0, my_z],
                 z_device(z_peer(d)),
             ).start()
 
     def square_mid(i):
         for d in range(1, ZS):
             z = z_peer(d)
-            got = rcopy(pa.at[i, z], pa.at[i, z], p_s.at[i, 0, d], p_r.at[i, 0, z], z_device(z))
+            got = rcopy(pa.at[i, z], pa.at[i, z], s_s.at[d], p_r.at[i, 0, z], z_device(z))
             got.wait_recv()
             got.wait_send()
         total = pa[i, 0]
@@ -246,7 +246,7 @@
         pb[i, my_yx] = total
         for d in range(1, YXS):
             rcopy(
-                pb.at[i, my_yx], pb.at[i, my_yx], p_s.at[i, 1, d], p_r.at[i, 1, my_yx],
+                pb.at[i, my_yx], pb.at[i, my_yx], s_s.at[d], p_r.at[i, 1, my_yx],
                 yx_device(yx_peer(d)),
             ).start()
 
@@ -254,7 +254,7 @@
         for d in range(1, YXS):
             yx = yx_peer(d)
             got = rcopy(
-                pb.at[i, yx], pb.at[i, yx], p_s.at[i, 1, d], p_r.at[i, 1, yx], yx_device(yx)
+                pb.at[i, yx], pb.at[i, yx], s_s.at[d], p_r.at[i, 1, yx], yx_device(yx)
             )
             got.wait_recv()
             got.wait_send()
@@ -302,29 +302,33 @@
         return out
 
     def hessian(h, q):
+        terms = 2 if h > 0 else 1
         parts = []
         for b in q:
-            parts += list(split(b))
+            parts += list(split(b))[:terms]
         cells = jnp.concatenate(parts, axis=0).astype(BF16)
 
         def gather_cells(m):
             got = dot(cells, ohc[:, pl.ds(mo(m * 256, 256), 256)])
             a = ac8[pl.ds(mo(m * 8, 8), 8), :]
-            g = jnp.where(
-                a == 0,
-                got[0:8] + got[8:16],
-                jnp.where(a == 1, got[16:24] + got[24:32], got[32:40] + got[40:48]),
-            )
+            level = []
+            for n in range(3):
+                r = n * 8 * terms
+                level.append(got[r : r + 8] + got[r + 8 : r + 16] if h > 0 else got[r : r + 8])
+            g = jnp.where(a == 0, level[0], jnp.where(a == 1, level[1], level[2]))
             hi, lo = split(g)
             rows = pl.ds(mo(m * 16, 16), 16)
             gh[rows, :] = jnp.concatenate([hi[:, :128], hi[:, 128:]], axis=0).astype(BF16)
-            gl[rows, :] = jnp.concatenate([lo[:, :128], lo[:, 128:]], axis=0).astype(BF16)
+            if h > 0:
+                gl[rows, :] = jnp.concatenate([lo[:, :128], lo[:, 128:]], axis=0).astype(BF16)
 
         each(U_IN, gather_cells)
 
         for i in range(4):
             rows = slice(i * 64, i * 64 + 64)
-            wide = dot(gh[rows, :], rep[...]) + dot(gl[rows, :], rep[...])
+            wide = dot(gh[rows, :], rep[...])
+            if h > 0:
+                wide = wide + dot(gl[rows, :], rep[...])
             xin[rows, :] = (wide * fr8[rows, :]).astype(BF16)
 
         def forward(m):
@@ -495,7 +499,7 @@
             fp.at[group, :, span], landing.at[source], g_s.at[kind, d], g_r.at[kind, source], device
         )
 
-    order = [(kind, d) for d in range(GROUPS) for kind in range(3) if kind < 2 or d > 0]
+    order = [(kind, d) for kind in range(3) for d in range(GROUPS) if kind < 2 or d > 0]
     for kind, d in order:
         final(kind, d, group).start()
     for kind, d in order:
@@ -528,12 +532,12 @@
     for d in range(1, YXS):
         yx = yx_peer(d)
         rcopy(
-            gk.at[yx], ka.at[my_yx], k_s.at[0, d], k_r.at[0, my_yx],
+            gk.at[yx], ka.at[my_yx], s_s.at[d], k_r.at[0, my_yx],
             yx_device(yx),
         ).start()
     for d in range(1, YXS):
         yx = yx_peer(d)
-        got = rcopy(ka.at[yx], ka.at[yx], k_s.at[0, d], k_r.at[0, yx], yx_device(yx))
+        got = rcopy(ka.at[yx], ka.at[yx], s_s.at[d], k_r.at[0, yx], yx_device(yx))
         got.wait_recv()
         got.wait_send()
     ka[my_yx] = gk[my_yx]
@@ -543,11 +547,11 @@
     kb[my_z] = total.astype(BF16)
     for d in range(1, ZS):
         rcopy(
-            kb.at[my_z], kb.at[my_z], k_s.at[1, d], k_r.at[1, my_z], z_device(z_peer(d))
+            kb.at[my_z], kb.at[my_z], s_s.at[d], k_r.at[1, my_z], z_device(z_peer(d))
         ).start()
     for d in range(1, ZS):
         z = z_peer(d)
-        got = rcopy(kb.at[z], kb.at[z], k_s.at[1, d], k_r.at[1, z], z_device(z))
+        got = rcopy(kb.at[z], kb.at[z], s_s.at[d], k_r.at[1, z], z_device(z))
         got.wait_recv()
         got.wait_send()
     total = kb[0].astype(F32)
@@ -556,16 +560,23 @@
     kc[my_yx] = total
     for d in range(1, YXS):
         rcopy(
-            kc.at[my_yx], kc.at[my_yx], k_s.at[2, d], k_r.at[2, my_yx], yx_device(yx_peer(d))
+            kc.at[my_yx], kc.at[my_yx], s_s.at[d], k_r.at[2, my_yx], yx_device(yx_peer(d))
         ).start()
     for d in range(1, YXS):
         yx = yx_peer(d)
-        got = rcopy(kc.at[yx], kc.at[yx], k_s.at[2, d], k_r.at[2, yx], yx_device(yx))
+        got = rcopy(kc.at[yx], kc.at[yx], s_s.at[d], k_r.at[2, yx], yx_device(yx))
         got.wait_recv()
         got.wait_send()
     for yx in range(YXS):
         gram_ref[yx * 8 : yx * 8 + 8, 0:128] = kc[yx, 0:8]
         gram_ref[yx * 8 : yx * 8 + 8, 128:256] = kc[yx, 8:16]
+
+
+def finish(cells_ref, sums_ref, samp_ref, refd_ref, gram_ref):
+    samp_ref[...] = cells_ref[0:8, :]
+    refd_ref[...] = cells_ref[8:16, :]
+    for j in range(2):
+        gram_ref[j * 128 : j * 128 + 128, :] = jnp.transpose(sums_ref[:, j * 128 : j * 128 + 128])
 
 
 def shards(
@@ -644,11 +655,10 @@
             dma((ROUNDS, 2)),
             dma((ROUNDS, 2)),
             dma((ROUNDS, 2)),
-            dma((POWER, 2, 8)),
+            dma((8,)),
             dma((POWER, 2, 8)),
             dma((3, GROUPS)),
             dma((3, GROUPS)),
-            dma((3, 8)),
             dma((3, 8)),
         ],
         compiler_params=pltpu.CompilerParams(
@@ -658,7 +668,17 @@
         blocks, connectivity, basal_map, friction.transpose(2, 0, 1), elem_counts,
         obs_weight.T, sign_bits.T, cluster_ids[None, :],
     )
-    return cells[:8].T, cells[8:].T, gram.reshape(64, 8, 32)
+    samp, refd, gram = pl.pallas_call(
+        finish,
+        out_shape=(
+            jax.ShapeDtypeStruct((8, 256), F32),
+            jax.ShapeDtypeStruct((8, 256), F32),
+            jax.ShapeDtypeStruct((256, 64), F32),
+        ),
+        in_specs=[vmem, vmem],
+        out_specs=(vmem, vmem, vmem),
+    )(cells, gram)
+    return samp.T, refd.T, gram.reshape(8, 32, 64).transpose(2, 0, 1)
 
 
 def solution(mesh):

time: 78.8 us -> 75.9 us (0.963)
  local copies, waits for them, and re-layouts: 2.91 us -> 0 us
    pallas_call x1, Pallas kernels: 74.3 us -> 72.7 us  [shards(): pl.pallas_call(kernel, out_shape=(jax.ShapeDtypeStruct((16, 256), F32), j...]
    pallas_call x0 -> x1, Pallas kernels: none -> 1.61 us  [shards(): pl.pallas_call(finish, out_shape=(jax.ShapeDtypeStruct((8, 256), F32), ja...]
    pallas_call x1 -> x0, local copies, waits for them, and re-layouts: 1.59 us -> none  [shards(): pl.pallas_call(kernel, out_shape=(jax.ShapeDtypeStruct((16, 256), F32), j...]
    transpose x1 -> x0, local copies, waits for them, and re-layouts: 1.32 us -> none  [shards(): return (cells[:8].T, cells[8:].T, gram.reshape(64, 8, 32))]
where the time goes in v5:
time: 75.9 us; the launch traced here: 75.6 us
  Pallas kernels  74.3 us (98%)
  between operations  1.29 us (2%)
    pallas_call x1, Pallas kernels, shards(): pl.pallas_call(kernel, out_shape=(jax.ShapeDtypeStruct((16, 256), F32), j...  72.7 us
    pallas_call x1, Pallas kernels, shards(): pl.pallas_call(finish, out_shape=(jax.ShapeDtypeStruct((8, 256), F32), ja...  1.61 us

profile of v5, /device:TPU:2, one launch (start us, length us, event | category | flops | bytes accessed | tf_op | source)
XLA Modules:
  0.0 75.6 jit_solution(15734153259697844678)
XLA Ops:
  1.3 72.7 %shard_map.103 = (f32[16,256]{1,0:T(8,128)}, f32[64,256]{1,0:T(8,128)}) custom-call(bf16[64,192,192]{2,1,0:T(8,128)(2,1)} %blk_hbm.1, s32[64,64]{1,0:T(8,128)} %conn_hbm.1, s32[64,64]{1,0:T(8,128)} %cell_hbm.1, f32[3,64,64]{2,1,0:T(8,128)} %bitcast.9, s32[1]{0:T(128)S(6)} %copy.11.count_ref, f32[3,4096]{1,0:T(4,128)} %bitcast.10, s32[8,256]{1,0:T(8,128)} %bitcast.11, ...), custom_call_target="tpu_custom_call" | custom-call | tf_op jit(solution)/shard_map/pallas_call | solution.py:588
  73.9 1.6 %shard_map.104 = (f32[8,256]{1,0:T(8,128)}, f32[8,256]{1,0:T(8,128)}, f32[256,64]{1,0:T(8,128)}) custom-call(f32[16,256]{1,0:T(8,128)} %get-tuple-element.8.cells_ref, f32[64,256]{1,0:T(8,128)} %get-tuple-element.9.sums_ref), custom_call_target="tpu_custom_call" | custom-call | tf_op jit(solution)/shard_map/pallas_call | solution.py:671

commit v6 on v5

--- a/solution.py
+++ b/solution.py
@@ -19,7 +19,6 @@
 CHUNKS = 16
 U_IN = 16
 U_PROD = 16
-U_EDGE = 8
 U_INNER = 8
 U_GET = 4
 U_PUT = 16
@@ -34,10 +33,15 @@
 
 
 def mo(x, n):
-    return pl.multiple_of(x, n)
+    return x if isinstance(x, int) else pl.multiple_of(x, n)
 
 
 def each(unroll, body, steps=CHUNKS):
+    if unroll == steps:
+        for j in range(steps):
+            body(j)
+        return
+
     @pl.loop(0, steps // unroll)
     def _(n):
         for j in range(unroll):
@@ -346,14 +350,11 @@
             rows = slice(i * 64, i * 64 + 64)
             fc[rows, :] = dot(fw[rows, :], pmt[...])
 
-        acce[...] = jnp.zeros(acce.shape, F32)
         acci[...] = jnp.zeros(acci.shape, F32)
 
-        @pl.loop(0, CHUNKS // U_EDGE)
-        def _(n):
-            acce[...] += scatter_nodes(n, U_EDGE, EDGE)
-
-        esend[h] = acce[...].astype(BF16)
+        edges = scatter_nodes(0, CHUNKS, EDGE)
+        acce[...] = edges
+        esend[h] = edges.astype(BF16)
         swap = [
             rcopy(esend.at[h, pl.ds(0, 48), :], renext.at[h], e_s.at[h, 0], e_r.at[h, 0], (prv, group)),
             rcopy(esend.at[h, pl.ds(48, 48), :], reprev.at[h], e_s.at[h, 1], e_r.at[h, 1], (nxt, group)),
@@ -416,7 +417,7 @@
                     [out[c][:, j * 128 : j * 128 + 128] for j in range(4)], axis=0
                 ).astype(BF16)
 
-        each(U_GET, gather_edge, CHUNKS // 2)
+        each(CHUNKS // 2, gather_edge, CHUNKS // 2)
 
         for i in range(4):
             rows = slice(i * 64, i * 64 + 64)

time: 75.9 us -> 75.1 us (0.989)
  Pallas kernels: 74.3 us -> 73.5 us
where the time goes in v6:
time: 75.1 us; the launch traced here: 74.8 us
  Pallas kernels  73.5 us (98%)
  between operations  1.29 us (2%)
    pallas_call x1, Pallas kernels, shards(): pl.pallas_call(kernel, out_shape=(jax.ShapeDtypeStruct((16, 256), F32), j...  71.9 us
    pallas_call x1, Pallas kernels, shards(): pl.pallas_call(finish, out_shape=(jax.ShapeDtypeStruct((8, 256), F32), ja...  1.61 us

profile of v6, /device:TPU:2, one launch (start us, length us, event | category | flops | bytes accessed | tf_op | source)
XLA Modules:
  0.0 74.8 jit_solution(14912369317374652971)
XLA Ops:
  1.3 71.9 %shard_map.103 = (f32[16,256]{1,0:T(8,128)}, f32[64,256]{1,0:T(8,128)}) custom-call(bf16[64,192,192]{2,1,0:T(8,128)(2,1)} %blk_hbm.1, s32[64,64]{1,0:T(8,128)} %conn_hbm.1, s32[64,64]{1,0:T(8,128)} %cell_hbm.1, f32[3,64,64]{2,1,0:T(8,128)} %bitcast.9, s32[1]{0:T(128)S(6)} %copy.11.count_ref, f32[3,4096]{1,0:T(4,128)} %bitcast.10, s32[8,256]{1,0:T(8,128)} %bitcast.11, ...), custom_call_target="tpu_custom_call" | custom-call | tf_op jit(solution)/shard_map/pallas_call | solution.py:589
  73.2 1.6 %shard_map.104 = (f32[8,256]{1,0:T(8,128)}, f32[8,256]{1,0:T(8,128)}, f32[256,64]{1,0:T(8,128)}) custom-call(f32[16,256]{1,0:T(8,128)} %get-tuple-element.8.cells_ref, f32[64,256]{1,0:T(8,128)} %get-tuple-element.9.sums_ref), custom_call_target="tpu_custom_call" | custom-call | tf_op jit(solution)/shard_map/pallas_call | solution.py:672

commit v7 on v6

--- a/solution.py
+++ b/solution.py
@@ -63,8 +63,8 @@
     conn, cell, fr3, w3, sign, cl_ref, idx_ref, qs_ref,
     blk, ohn, ohnt, ohc, ohct, an8, ac8, fr8, rep, sel, pm, pmt,
     gh, gl, xin, fw, fc, acce, acci, te, ti, ad1, ad, ain, yh, yl, pt,
-    wn, qsp, qsn, esend, renext, reprev, bs, rbn, rbp, pa, pb, fp, fpn, fpp, gk, ka, kb, kc,
-    blk_sem, in_sem, i_s, i_r, e_s, e_r, b_s, b_r, s_s, p_r, g_s, g_r, k_r,
+    wn, qsp, qsn, esend, renext, reprev, bs, rbn, rbp, pa, pb, fp, fpn, fpp, gk, ka, kb, kc, cells_v,
+    blk_sem, in_sem, out_sem, i_s, i_r, e_s, e_r, b_s, b_r, s_s, p_r, g_s, g_r, k_r,
 ):
     tile = lax.axis_index("tiles")
     group = lax.axis_index("probes")
@@ -206,7 +206,7 @@
         ohnt[span, :] = one(lane_n == cols[:, i : i + 1])
         ohct[span, :] = one(lane_c == cols[:, PAIRS + i : PAIRS + i + 1])
 
-    for cpy in first:
+    for cpy in first[:2]:
         cpy.wait()
     load.wait()
 
@@ -387,7 +387,7 @@
 
         each(U_GET, gather_inner, CHUNKS // 2)
 
-        for cpy in swap:
+        for cpy in swap if h > 0 else swap + first[2:]:
             cpy.wait()
         for i in range(6):
             if i < 3:
@@ -488,7 +488,7 @@
         if h < POWER:
             square_start(h, q)
         if h == 0:
-            out_ref[0:8, :] = pltpu.roll(jnp.concatenate(q, axis=1), 384 - RIM, 1)[:, :256]
+            cells_v[0:8, :] = pltpu.roll(jnp.concatenate(q, axis=1), 384 - RIM, 1)[:, :256]
     def final(kind, d, source):
         other = lax.rem(group + d, GROUPS)
         device, landing, span = (
@@ -519,7 +519,9 @@
         )
 
     mine = pltpu.roll(window(group), 384 - RIM, 1)[:, :256]
-    out_ref[8:16, :] = mine
+    cells_v[8:16, :] = mine
+    put = pltpu.make_async_copy(cells_v, out_ref, out_sem.at[0])
+    put.start()
     every = jnp.concatenate([window(g) for g in range(GROUPS)], axis=0)
     every = pltpu.roll(every, 384 - RIM, 1)[:, :256]
     outer = jnp.concatenate([every * mine[i : i + 1, :] for i in range(8)], axis=0)
@@ -558,26 +560,28 @@
     total = kb[0].astype(F32)
     for z in range(1, ZS):
         total = total + kb[z].astype(F32)
-    kc[my_yx] = total
+    kc[...] = total
+    keep = pltpu.make_async_copy(kc, gram_ref.at[my_yx], out_sem.at[1])
     for d in range(1, YXS):
         rcopy(
-            kc.at[my_yx], kc.at[my_yx], s_s.at[d], k_r.at[2, my_yx], yx_device(yx_peer(d))
+            kc, gram_ref.at[my_yx], s_s.at[d], k_r.at[2, my_yx], yx_device(yx_peer(d))
         ).start()
+    keep.start()
     for d in range(1, YXS):
         yx = yx_peer(d)
-        got = rcopy(kc.at[yx], kc.at[yx], s_s.at[d], k_r.at[2, yx], yx_device(yx))
+        got = rcopy(kc, gram_ref.at[yx], s_s.at[d], k_r.at[2, yx], yx_device(yx))
         got.wait_recv()
         got.wait_send()
-    for yx in range(YXS):
-        gram_ref[yx * 8 : yx * 8 + 8, 0:128] = kc[yx, 0:8]
-        gram_ref[yx * 8 : yx * 8 + 8, 128:256] = kc[yx, 8:16]
+    keep.wait()
+    put.wait()
 
 
 def finish(cells_ref, sums_ref, samp_ref, refd_ref, gram_ref):
     samp_ref[...] = cells_ref[0:8, :]
     refd_ref[...] = cells_ref[8:16, :]
     for j in range(2):
-        gram_ref[j * 128 : j * 128 + 128, :] = jnp.transpose(sums_ref[:, j * 128 : j * 128 + 128])
+        rows = jnp.concatenate([sums_ref[n, j * 8 : j * 8 + 8] for n in range(YXS)], axis=0)
+        gram_ref[j * 128 : j * 128 + 128, :] = jnp.transpose(rows)
 
 
 def shards(
@@ -590,10 +594,10 @@
         kernel,
         out_shape=(
             jax.ShapeDtypeStruct((16, 256), F32),
-            jax.ShapeDtypeStruct((64, 256), F32),
+            jax.ShapeDtypeStruct((YXS, 16, 128), F32),
         ),
         in_specs=[here] * 4 + [pl.BlockSpec(memory_space=pltpu.SMEM)] + [here] * 3,
-        out_specs=(vmem, vmem),
+        out_specs=(here, here),
         scratch_shapes=[
             pltpu.VMEM((ELEMS, 64), I32),
             pltpu.VMEM((ELEMS, 64), I32),
@@ -647,9 +651,11 @@
             pltpu.VMEM((YXS, 16, 128), BF16),
             pltpu.VMEM((YXS, 16, 128), BF16),
             pltpu.VMEM((ZS, 16, 128), BF16),
-            pltpu.VMEM((YXS, 16, 128), F32),
+            pltpu.VMEM((16, 128), F32),
+            pltpu.VMEM((16, 256), F32),
             dma,
             dma((6,)),
+            dma((2,)),
             dma((3,)),
             dma((3,)),
             dma((ROUNDS, 2)),

time: 75.1 us -> 74.5 us (level)
  no operation moved by 1% of the time
where the time goes in v7:
time: 74.5 us; the launch traced here: 74.2 us
  Pallas kernels  72.9 us (98%)
  between operations  1.29 us (2%)
    pallas_call x1, Pallas kernels, shards(): pl.pallas_call(kernel, out_shape=(jax.ShapeDtypeStruct((16, 256), F32), j...  71.3 us
    pallas_call x1, Pallas kernels, shards(): pl.pallas_call(finish, out_shape=(jax.ShapeDtypeStruct((8, 256), F32), ja...  1.61 us

profile of v7, /device:TPU:2, one launch (start us, length us, event | category | flops | bytes accessed | tf_op | source)
XLA Modules:
  0.0 74.2 jit_solution(5951956941756423831)
XLA Ops:
  1.3 71.3 %shard_map.103 = (f32[16,256]{1,0:T(8,128)}, f32[8,16,128]{2,1,0:T(8,128)}) custom-call(bf16[64,192,192]{2,1,0:T(8,128)(2,1)} %blk_hbm.1, s32[64,64]{1,0:T(8,128)} %conn_hbm.1, s32[64,64]{1,0:T(8,128)} %cell_hbm.1, f32[3,64,64]{2,1,0:T(8,128)} %bitcast.9, s32[1]{0:T(128)S(6)} %copy.11.count_ref, f32[3,4096]{1,0:T(4,128)} %bitcast.10, s32[8,256]{1,0:T(8,128)} %bitcast.11, ...), custom_call_target="tpu_custom_call" | custom-call | tf_op jit(solution)/shard_map/pallas_call | solution.py:593
  72.6 1.6 %shard_map.104 = (f32[8,256]{1,0:T(8,128)}, f32[8,256]{1,0:T(8,128)}, f32[256,64]{1,0:T(8,128)}) custom-call(f32[16,256]{1,0:T(8,128)} %get-tuple-element.8.cells_ref, f32[8,16,128]{2,1,0:T(8,128)} %get-tuple-element.9.sums_ref), custom_call_target="tpu_custom_call" | custom-call | tf_op jit(solution)/shard_map/pallas_call | solution.py:678

commit v8 on v7

--- a/solution.py
+++ b/solution.py
@@ -21,7 +21,6 @@
 U_PROD = 16
 U_INNER = 8
 U_GET = 4
-U_PUT = 16
 ZS = 8
 YXS = 8
 GROUPS = 4
@@ -440,24 +439,24 @@
             rows = slice(i * 64, i * 64 + 64)
             pt[rows, :] = dot(yh[rows, :], sel[...]) + dot(yl[rows, :], sel[...])
 
-        def scatter_cells(n, acc):
+        def scatter_cells(levels):
             spreads = []
-            for j in range(U_PUT):
-                m = n * U_PUT + j
-                r0 = mo(m * 16, 16)
-                v = jnp.concatenate([pt[pl.ds(r0, 8), :], pt[pl.ds(r0 + 8, 8), :]], axis=1)
-                a = ac8[pl.ds(mo(m * 8, 8), 8), :]
+            for m in range(CHUNKS):
+                r0 = m * 16
+                v = jnp.concatenate([pt[r0 : r0 + 8, :], pt[r0 + 8 : r0 + 16, :]], axis=1)
+                a = ac8[m * 8 : m * 8 + 8, :]
                 spread = jnp.concatenate(
-                    [jnp.where(a == lv, s, 0.0) for lv in range(3) for s in split(v)], axis=0
+                    [jnp.where(a == lv, s, 0.0) for lv in levels for s in split(v)], axis=0
                 )
                 spreads.append(spread.astype(BF16))
-            size = U_PUT * 256
-            return acc + dot(
-                jnp.concatenate(spreads, axis=1), ohct[pl.ds(mo(n * size, size), size), :]
-            )
-
-        acc = lax.fori_loop(0, CHUNKS // U_PUT, scatter_cells, jnp.zeros((48, 128), F32))
-        sums = [acc[n * 16 : n * 16 + 8] + acc[n * 16 + 8 : n * 16 + 16] for n in range(3)]
+            acc = dot(jnp.concatenate(spreads, axis=1), ohct[...])
+            return [acc[n * 16 : n * 16 + 8] + acc[n * 16 + 8 : n * 16 + 16] for n in range(len(levels))]
+
+        if h == POWER:
+            sums = scatter_cells((0, 1, 2))
+        else:
+            before, after = scatter_cells((0, 2))
+            sums = [before, None, after]
         keep = same if h % 2 == 1 else [exist[n] - same[n] for n in range(3)]
         if h == POWER:
             scale = square_end(h - 1)
@@ -472,6 +471,7 @@
         ]
         for cpy in swap:
             cpy.start()
+        sums[1] = scatter_cells((1,))[0]
         scale = square_end(h - 1) if h > 0 else None
         for cpy in swap:
             cpy.wait()
@@ -525,9 +525,8 @@
     every = jnp.concatenate([window(g) for g in range(GROUPS)], axis=0)
     every = pltpu.roll(every, 384 - RIM, 1)[:, :256]
     outer = jnp.concatenate([every * mine[i : i + 1, :] for i in range(8)], axis=0)
-    hi, lo = split(outer)
     member = one(lax.broadcasted_iota(I32, (64, 256), 0) == cl_ref[...])
-    grams = dot(member, hi.astype(BF16), NT) + dot(member, lo.astype(BF16), NT)
+    grams = dot(member, outer.astype(BF16), NT)
     for yx in range(YXS):
         rows = grams[yx * 8 : yx * 8 + 8]
         gk[yx] = jnp.concatenate([rows[:, :128], rows[:, 128:]], axis=0).astype(BF16)

time: 74.5 us -> 74.4 us (level)
  no operation moved by 1% of the time
where the time goes in v8:
time: 74.4 us; the launch traced here: 74.2 us
  Pallas kernels  72.9 us (98%)
  between operations  1.29 us (2%)
    pallas_call x1, Pallas kernels, shards(): pl.pallas_call(kernel, out_shape=(jax.ShapeDtypeStruct((16, 256), F32), j...  71.3 us
    pallas_call x1, Pallas kernels, shards(): pl.pallas_call(finish, out_shape=(jax.ShapeDtypeStruct((8, 256), F32), ja...  1.61 us

profile of v8, /device:TPU:2, one launch (start us, length us, event | category | flops | bytes accessed | tf_op | source)
XLA Modules:
  0.0 74.2 jit_solution(13533773244750036414)
XLA Ops:
  1.3 71.3 %shard_map.103 = (f32[16,256]{1,0:T(8,128)}, f32[8,16,128]{2,1,0:T(8,128)}) custom-call(bf16[64,192,192]{2,1,0:T(8,128)(2,1)} %blk_hbm.1, s32[64,64]{1,0:T(8,128)} %conn_hbm.1, s32[64,64]{1,0:T(8,128)} %cell_hbm.1, f32[3,64,64]{2,1,0:T(8,128)} %bitcast.9, s32[1]{0:T(128)S(6)} %copy.11.count_ref, f32[3,4096]{1,0:T(4,128)} %bitcast.10, s32[8,256]{1,0:T(8,128)} %bitcast.11, ...), custom_call_target="tpu_custom_call" | custom-call | tf_op jit(solution)/shard_map/pallas_call | solution.py:592
  72.6 1.6 %shard_map.104 = (f32[8,256]{1,0:T(8,128)}, f32[8,256]{1,0:T(8,128)}, f32[256,64]{1,0:T(8,128)}) custom-call(f32[16,256]{1,0:T(8,128)} %get-tuple-element.8.cells_ref, f32[8,16,128]{2,1,0:T(8,128)} %get-tuple-element.9.sums_ref), custom_call_target="tpu_custom_call" | custom-call | tf_op jit(solution)/shard_map/pallas_call | solution.py:677
